TPU v7x, 32 devices: a whole 2x2x4 slice. The times are simulated.
32 devices in a mesh: batch: 8 (over z, x), tensor: 4 (over y, core).
Axes of the slice: x: 2, y: 2, z: 4, core: 2. Of those that a mesh axis runs over, the one named last changes fastest.
Arguments:
- token_ids: int32 [8, 1024], P('batch'), may hold values from 0 to 50303
- targets: int32 [8, 1024], P('batch'), may hold values from 0 to 50303
- task_groups: int32 [8], P('batch'), may hold values from 0 to 3, as said below
- embedding: bfloat16 [50304, 1024], P('tensor'), may hold values from -0.3984375 to 0.3984375
- positions: bfloat16 [1024, 1024], replicated, may hold values from -0.59765625 to 0.59765625
- norm_gains: float32 [3, 1024], replicated, may hold values from 0.5 to 1.5
- norm_shifts: float32 [3, 1024], replicated, may hold values from -1.2 to 1.2
- w_qkv: bfloat16 [1024, 3, 1024], P(None, None, 'tensor'), may hold values from -0.1875 to 0.1875
- attention_output_weight: bfloat16 [1024, 1024], P('tensor'), may hold values from -0.375 to 0.375
- expand_weight: bfloat16 [1024, 4096], P(None, 'tensor'), may hold values from -0.1875 to 0.1875
- contract_weight: bfloat16 [4096, 1024], P('tensor'), may hold values from -0.046875 to 0.046875
- model_down_maps: float32 [5, 1024, 4], replicated, may hold values from -0.1875 to 0.1875
- hidden_down_map: float32 [4096, 4], replicated, may hold values from -0.09375 to 0.09375
- model_up_maps: float32 [5, 4, 1024], replicated, may hold values from -0.18 to 0.18
- hidden_up_map: float32 [4, 4096], replicated, may hold values from -0.18 to 0.18
- model_down_first: float32 [5, 1024, 4], replicated, may hold values from -5.722046e-06 to 5.722046e-06
- hidden_down_first: float32 [4096, 4], replicated, may hold values from -5.722046e-06 to 5.722046e-06
- model_up_first: float32 [5, 4, 1024], replicated, may hold values from -5.722046e-06 to 5.722046e-06
- hidden_up_first: float32 [4, 4096], replicated, may hold values from -5.722046e-06 to 5.722046e-06
- model_down_second: float32 [5, 1024, 4], replicated, may hold values from 1.3563368e-14 to 5.4253473e-14
- hidden_down_second: float32 [4096, 4], replicated, may hold values from 1.3563368e-14 to 5.4253473e-14
- model_up_second: float32 [5, 4, 1024], replicated, may hold values from 1.3563368e-14 to 5.4253473e-14
- hidden_up_second: float32 [4, 4096], replicated, may hold values from 1.3563368e-14 to 5.4253473e-14
Outputs:
- loss: float32 [], replicated
- grad_norm: float32 [], replicated
- a_model_new: float32 [5, 1024, 4], replicated
- a_hidden_new: float32 [4096, 4], replicated
- b_model_new: float32 [5, 4, 1024], replicated
- b_hidden_new: float32 [4, 4096], replicated
- a_model_m_new: float32 [5, 1024, 4], replicated
- a_hidden_m_new: float32 [4096, 4], replicated
- b_model_m_new: float32 [5, 4, 1024], replicated
- b_hidden_m_new: float32 [4, 4096], replicated
- a_model_v_new: float32 [5, 1024, 4], replicated
- a_hidden_v_new: float32 [4096, 4], replicated
- b_model_v_new: float32 [5, 4, 1024], replicated
- b_hidden_v_new: float32 [4, 4096], replicated
Inputs may be any that keep to these rules, and one draw needn't show every extreme that they name: `task_groups`: every one of the 4 groups holds at least one sequence.
All inputs are finite; a program needn't handle non-finite values.
Results may differ from a plain program's by a relative error of at most 0.0038.
Values may be sent and summed in bfloat16 or wider, within the bound.
No kernel may reach another device: no remote copies, remote signals or barrier semaphores. Data moves between devices by JAX's collectives and lax.ppermute only.
A program may use at most 192 MiB of HBM per device.

v0:
```python
import math

import jax
import jax.numpy as jnp
from jax import lax
from jax.sharding import PartitionSpec as P

HEAD_DIM = 64
GROUPS = 4
ADAM_STEP = 5


highest_accuracy = lax.Precision.HIGHEST
beta_one = 0.9
beta_two = 0.999
learn_rate = 0.01
decay_rate = 0.01
adam_eps = 1e-08
clip_limit = 0.001
adapter_scale = 8.0


def layer_norm(values, scales, shifts):
    centre = jnp.mean(values, -1, keepdims=True)
    centred = values - centre
    spread = jnp.mean(centred * centred, -1, keepdims=True)
    return centred * lax.rsqrt(spread + 1e-05) * scales + shifts


def norm_back(values, scales, shifts, upstream):
    pullback = jax.vjp(lambda inner: layer_norm(inner, scales, shifts), values)[1]
    return pullback(upstream)[0]


def gelu(values):
    return (
        0.5
        * values
        * (1.0 + jnp.tanh(0.7978845608028654 * (values + 0.044715 * values * values * values)))
    )


def plain_product(left, right):
    return jnp.dot(left, right, preferred_element_type=jnp.float32)


def plain_transposed(left, right):
    return lax.dot_general(
        left, right, (((1,), (1,)), ((), ())), preferred_element_type=jnp.float32
    )


def precise_product(left, right):
    return jnp.dot(left, right, precision=highest_accuracy, preferred_element_type=jnp.float32)


def adam_update(weight, grad, first, second):
    first = beta_one * first + (1.0 - beta_one) * grad
    second = beta_two * second + (1.0 - beta_two) * grad * grad
    first_fix = 1.0 - beta_one**ADAM_STEP
    second_fix = 1.0 - beta_two**ADAM_STEP
    stride = first / first_fix / (jnp.sqrt(second / second_fix) + adam_eps)
    return (weight - learn_rate * (stride + decay_rate * weight), first, second)


def masked_scores(seq_block, queries, row_start, block_rows, score_scale):
    scores = (
        jnp.einsum("qhd,khd->hqk", queries, seq_block[:, 1], preferred_element_type=jnp.float32)
        * score_scale
    )
    causal = (row_start + jnp.arange(block_rows))[:, None] >= jnp.arange(seq_block.shape[0])[
        None, :
    ]
    return jnp.where(causal[None], scores, -1e30)


def attention_forward(packed_arrays, block_rows, score_scale):
    per_seq = packed_arrays.shape[1] // block_rows

    def one_block(block_index):
        seq_index = block_index // per_seq
        row_start = block_index % per_seq * block_rows
        seq_block = lax.dynamic_index_in_dim(packed_arrays, seq_index, 0, keepdims=False)
        queries = lax.dynamic_slice_in_dim(seq_block[:, 0], row_start, block_rows, 0)
        scores = masked_scores(seq_block, queries, row_start, block_rows, score_scale)
        row_peak = jnp.max(scores, -1)
        raised = jnp.exp(scores - row_peak[..., None])
        row_total = jnp.sum(raised, -1)
        weights_b = (raised / row_total[..., None]).astype(jnp.bfloat16)
        mixed_out = jnp.einsum(
            "hqk,khd->qhd", weights_b, seq_block[:, 2], preferred_element_type=jnp.float32
        )
        return (mixed_out.astype(jnp.bfloat16), row_peak + jnp.log(row_total))

    return lax.map(one_block, jnp.arange(packed_arrays.shape[0] * per_seq))


def attention_backward(packed_arrays, log_totals, grad_out, block_rows, score_scale):
    per_seq = packed_arrays.shape[1] // block_rows

    def one_block(block_index, running):
        seq_index = block_index // per_seq
        row_start = block_index % per_seq * block_rows
        seq_block = lax.dynamic_index_in_dim(packed_arrays, seq_index, 0, keepdims=False)
        queries = lax.dynamic_slice_in_dim(seq_block[:, 0], row_start, block_rows, 0)
        grad_rows = lax.dynamic_slice_in_dim(
            lax.dynamic_index_in_dim(grad_out, seq_index, 0, keepdims=False),
            row_start,
            block_rows,
            0,
        )
        scores = masked_scores(seq_block, queries, row_start, block_rows, score_scale)
        weights_f = jnp.exp(scores - log_totals[block_index][..., None])
        weights_b = weights_f.astype(jnp.bfloat16)
        grad_weights = jnp.einsum(
            "qhd,khd->hqk", grad_rows, seq_block[:, 2], preferred_element_type=jnp.float32
        )
        inner = jnp.sum(weights_f * grad_weights, -1, keepdims=True)
        grad_scores = (weights_f * (grad_weights - inner)).astype(jnp.bfloat16)
        grad_query = (
            jnp.einsum(
                "hqk,khd->qhd", grad_scores, seq_block[:, 1], preferred_element_type=jnp.float32
            )
            * score_scale
        )
        grad_key = (
            jnp.einsum("hqk,qhd->khd", grad_scores, queries, preferred_element_type=jnp.float32)
            * score_scale
        )
        grad_value = jnp.einsum(
            "hqk,qhd->khd", weights_b, grad_rows, preferred_element_type=jnp.float32
        )
        current = lax.dynamic_index_in_dim(running, seq_index, 0, keepdims=False)
        new_query = lax.dynamic_update_slice_in_dim(current[:, 0], grad_query, row_start, 0)
        current = jnp.stack([new_query, current[:, 1] + grad_key, current[:, 2] + grad_value], 1)
        return lax.dynamic_update_index_in_dim(running, current, seq_index, 0)

    return lax.fori_loop(
        0, packed_arrays.shape[0] * per_seq, one_block, jnp.zeros(packed_arrays.shape, jnp.float32)
    )


def shards(
    token_ids,
    targets,
    task_groups,
    embedding,
    positions,
    norm_gains,
    norm_shifts,
    w_qkv,
    attention_output_weight,
    expand_weight,
    contract_weight,
    model_down_maps,
    hidden_down_map,
    model_up_maps,
    hidden_up_map,
    model_down_first,
    hidden_down_first,
    model_up_first,
    hidden_up_first,
    model_down_second,
    hidden_down_second,
    model_up_second,
    hidden_up_second,
):
    worker_position = lax.axis_index("tensor")
    seq_count, length = token_ids.shape
    row_count = seq_count * length
    vocab_local = embedding.shape[0]
    feature_width = embedding.shape[1]
    feature_width_part = attention_output_weight.shape[0]
    hidden_local = expand_weight.shape[1]
    adapter_rank = model_down_maps.shape[2]
    head_local = feature_width_part // HEAD_DIM
    score_scale = HEAD_DIM ** (-0.5)
    is_first = worker_position == 0
    side_owner = jnp.where(is_first, 1.0, 0.0).astype(jnp.float32)

    def narrow_gradients(rows):
        return lax.psum(rows, "tensor")

    local_ids = token_ids.reshape(row_count) - worker_position * vocab_local
    inside = (local_ids >= 0) & (local_ids < vocab_local)
    looked = jnp.take(embedding, jnp.clip(local_ids, 0, vocab_local - 1), axis=0).astype(
        jnp.float32
    )
    looked = jnp.where(inside[:, None], looked, 0.0)
    pos_rows = jnp.tile(positions.astype(jnp.float32), (seq_count, 1))
    residual_embedded = (
        lax.psum(looked.astype(jnp.bfloat16), "tensor").astype(jnp.float32) + pos_rows
    )
    member = task_groups[:, None] == jnp.arange(GROUPS)[None, :]
    group_counts = lax.psum(jnp.sum(member.astype(jnp.int32), 0) * length, "batch")
    seq_weight = (
        jnp.sum(jnp.where(member, 1.0 / group_counts.astype(jnp.float32)[None, :], 0.0), 1) / GROUPS
    )
    row_weight = jnp.repeat(seq_weight, length)
    down_low_rows = model_down_maps.astype(jnp.bfloat16)
    down_output_part = lax.dynamic_slice_in_dim(
        down_low_rows[3], worker_position * feature_width_part, feature_width_part, 0
    )
    down_hidden_part = lax.dynamic_slice_in_dim(
        hidden_down_map, worker_position * hidden_local, hidden_local, 0
    ).astype(jnp.bfloat16)
    up_attention_part = lax.dynamic_slice_in_dim(
        model_up_maps[:3], worker_position * feature_width_part, feature_width_part, 2
    )
    up_hidden_part = lax.dynamic_slice_in_dim(
        hidden_up_map, worker_position * hidden_local, hidden_local, 1
    )
    first_normed = layer_norm(residual_embedded, norm_gains[0], norm_shifts[0]).astype(jnp.bfloat16)
    adapter_attention = jnp.einsum(
        "px,exl->pel", first_normed, down_low_rows[:3], preferred_element_type=jnp.float32
    )
    packed_arrays = jnp.einsum(
        "td,dcf->tcf", first_normed, w_qkv, preferred_element_type=jnp.float32
    )
    packed_arrays = packed_arrays + adapter_scale * jnp.einsum(
        "uqw,qwk->uqk", adapter_attention, up_attention_part, precision=highest_accuracy
    )
    packed_arrays = packed_arrays.astype(jnp.bfloat16).reshape(
        seq_count, length, 3, head_local, HEAD_DIM
    )
    block_rows = math.gcd(length, 512)
    attn_blocks, log_totals = attention_forward(packed_arrays, block_rows, score_scale)
    attention_output = attn_blocks.reshape(row_count, feature_width_part)
    residual_first, adapter_output = lax.psum(
        (
            plain_product(attention_output, attention_output_weight),
            plain_product(attention_output, down_output_part),
        ),
        "tensor",
    )
    residual_after_attention = (
        residual_embedded
        + residual_first
        + adapter_scale * precise_product(adapter_output, model_up_maps[3])
    )
    second_normed = layer_norm(residual_after_attention, norm_gains[1], norm_shifts[1]).astype(
        jnp.bfloat16
    )
    adapter_expand = plain_product(second_normed, down_low_rows[4])
    preactivation = plain_product(second_normed, expand_weight) + adapter_scale * precise_product(
        adapter_expand, up_hidden_part
    )
    activation = gelu(preactivation).astype(jnp.bfloat16)
    residual_second, adapter_contract = lax.psum(
        (plain_product(activation, contract_weight), plain_product(activation, down_hidden_part)),
        "tensor",
    )
    residual_after_mlp = (
        residual_after_attention
        + residual_second
        + adapter_scale * precise_product(adapter_contract, model_up_maps[4])
    )
    final_rows = layer_norm(residual_after_mlp, norm_gains[2], norm_shifts[2]).astype(jnp.bfloat16)
    vocab_rows = math.gcd(row_count, 512)
    vocab_blocks = row_count // vocab_rows
    local_targets = targets.reshape(row_count) - worker_position * vocab_local
    columns = jnp.arange(vocab_local)

    def block_logits(block_index):
        hidden_rows = lax.dynamic_slice_in_dim(final_rows, block_index * vocab_rows, vocab_rows, 0)
        wanted = lax.dynamic_slice_in_dim(local_targets, block_index * vocab_rows, vocab_rows, 0)
        return (plain_transposed(hidden_rows, embedding), columns[None, :] == wanted[:, None])

    def block_stats(block_index):
        logits, is_target = block_logits(block_index)
        row_peak = jnp.max(logits, -1)
        row_total = jnp.sum(jnp.exp(logits - row_peak[:, None]), -1)
        return (row_peak, row_total, jnp.sum(jnp.where(is_target, logits, 0.0), -1))

    row_peak, row_total, target_logit = lax.map(block_stats, jnp.arange(vocab_blocks))
    row_peak = row_peak.reshape(row_count)
    row_total = row_total.reshape(row_count)
    target_logit = target_logit.reshape(row_count)
    global_peak = lax.pmax(row_peak, "tensor")
    global_total, global_target = lax.psum(
        (row_total * jnp.exp(row_peak - global_peak), target_logit), "tensor"
    )
    log_total = global_peak + jnp.log(global_total)
    seq_loss = jnp.sum((log_total - global_target).reshape(seq_count, length), 1)
    loss_part = jnp.where(is_first, jnp.sum(seq_loss * seq_weight), 0.0)

    def block_back(block_index):
        logits, is_target = block_logits(block_index)
        rows_lse = lax.dynamic_slice_in_dim(log_total, block_index * vocab_rows, vocab_rows, 0)
        rows_weight = lax.dynamic_slice_in_dim(row_weight, block_index * vocab_rows, vocab_rows, 0)
        grad_logits = rows_weight[:, None] * (
            jnp.exp(logits - rows_lse[:, None]) - jnp.where(is_target, 1.0, 0.0)
        )
        return plain_product(grad_logits.astype(jnp.bfloat16), embedding)

    grad_final = narrow_gradients(
        lax.map(block_back, jnp.arange(vocab_blocks)).reshape(row_count, feature_width)
    )
    grad_two = norm_back(residual_after_mlp, norm_gains[2], norm_shifts[2], grad_final)
    gradient_second_low = grad_two.astype(jnp.bfloat16)
    gradient_up_contract = adapter_scale * precise_product(adapter_contract.T, gradient_second_low)
    gradient_adapter_contract = adapter_scale * precise_product(
        gradient_second_low, model_up_maps[4].T
    )
    gradient_down_hidden = precise_product(activation.T, gradient_adapter_contract)
    gradient_activation = plain_transposed(gradient_second_low, contract_weight) + precise_product(
        gradient_adapter_contract, down_hidden_part.T
    )
    gradient_preactivation = jax.vjp(gelu, preactivation)[1](gradient_activation)[0].astype(
        jnp.bfloat16
    )
    gradient_up_hidden = adapter_scale * precise_product(adapter_expand.T, gradient_preactivation)
    gradient_adapter_expand = adapter_scale * precise_product(
        gradient_preactivation, up_hidden_part.T
    )
    gradient_down_expand = precise_product(second_normed.T, gradient_adapter_expand)
    gradient_second_normed = narrow_gradients(
        plain_transposed(gradient_preactivation, expand_weight)
        + precise_product(gradient_adapter_expand, down_low_rows[4].T)
    )
    grad_one = grad_two + norm_back(
        residual_after_attention, norm_gains[1], norm_shifts[1], gradient_second_normed
    )
    gradient_first_low = grad_one.astype(jnp.bfloat16)
    gradient_up_output = adapter_scale * precise_product(adapter_output.T, gradient_first_low)
    gradient_adapter_output = adapter_scale * precise_product(
        gradient_first_low, model_up_maps[3].T
    )
    gradient_down_output = precise_product(attention_output.T, gradient_adapter_output)
    gradient_attention = (
        plain_transposed(gradient_first_low, attention_output_weight)
        + precise_product(gradient_adapter_output, down_output_part.T)
    ).astype(jnp.bfloat16)
    gradient_bundle = attention_backward(
        packed_arrays,
        log_totals,
        gradient_attention.reshape(seq_count, length, head_local, HEAD_DIM),
        block_rows,
        score_scale,
    )
    gradient_bundle = gradient_bundle.reshape(row_count, 3, feature_width_part)
    gradient_up_attention = adapter_scale * jnp.einsum(
        "cxw,cxp->xwp", adapter_attention, gradient_bundle, precision=highest_accuracy
    )
    gradient_adapter_attention = adapter_scale * jnp.einsum(
        "tjf,jrf->tjr", gradient_bundle, up_attention_part, precision=highest_accuracy
    )
    gradient_down_attention = jnp.einsum(
        "xv,xkg->kvg", first_normed, gradient_adapter_attention, precision=highest_accuracy
    )
    a_out_full = lax.dynamic_update_slice_in_dim(
        jnp.zeros((feature_width, adapter_rank), jnp.float32),
        gradient_down_output,
        worker_position * feature_width_part,
        0,
    )
    grad_a_model = jnp.concatenate(
        [gradient_down_attention, a_out_full[None], gradient_down_expand[None]], 0
    )
    grad_a_hidden = lax.dynamic_update_slice_in_dim(
        jnp.zeros(hidden_down_map.shape, jnp.float32),
        gradient_down_hidden,
        worker_position * hidden_local,
        0,
    )
    b_qkv_full = lax.dynamic_update_slice_in_dim(
        jnp.zeros((3, adapter_rank, feature_width), jnp.float32),
        gradient_up_attention,
        worker_position * feature_width_part,
        2,
    )
    b_rest = side_owner * jnp.stack([gradient_up_output, gradient_up_contract])
    grad_b_model = jnp.concatenate([b_qkv_full, b_rest], 0)
    grad_b_hidden = lax.dynamic_update_slice_in_dim(
        jnp.zeros(hidden_up_map.shape, jnp.float32),
        gradient_up_hidden,
        worker_position * hidden_local,
        1,
    )
    weights = (model_down_maps, hidden_down_map, model_up_maps, hidden_up_map)
    firsts = (model_down_first, hidden_down_first, model_up_first, hidden_up_first)
    seconds = (model_down_second, hidden_down_second, model_up_second, hidden_up_second)
    summed_a_model, summed_a_hidden, summed_b_model, summed_b_hidden, loss = lax.psum(
        (grad_a_model, grad_a_hidden, grad_b_model, grad_b_hidden, loss_part), ("batch", "tensor")
    )
    summed = (summed_a_model, summed_a_hidden, summed_b_model, summed_b_hidden)
    squares = jnp.sum(summed_a_model * summed_a_model) + jnp.sum(summed_a_hidden * summed_a_hidden)
    squares = (
        squares
        + jnp.sum(summed_b_model * summed_b_model)
        + jnp.sum(summed_b_hidden * summed_b_hidden)
    )
    grad_norm = jnp.sqrt(squares)
    factor = clip_limit / jnp.maximum(grad_norm, clip_limit)
    results = [
        adam_update(weights[place], summed[place] * factor, firsts[place], seconds[place])
        for place in range(4)
    ]
    outs_weight = tuple((result[0] for result in results))
    outs_first = tuple((result[1] for result in results))
    outs_second = tuple((result[2] for result in results))
    return (
        loss,
        grad_norm,
        outs_weight[0],
        outs_weight[1],
        outs_weight[2],
        outs_weight[3],
        outs_first[0],
        outs_first[1],
        outs_first[2],
        outs_first[3],
        outs_second[0],
        outs_second[1],
        outs_second[2],
        outs_second[3],
    )


def solution(mesh):
    return jax.shard_map(
        shards,
        mesh=mesh,
        in_specs=(
            P("batch", None),
            P("batch", None),
            P("batch"),
            P("tensor", None),
            P(),
            P(),
            P(),
            P(None, None, "tensor"),
            P("tensor", None),
            P(None, "tensor"),
            P("tensor", None),
            P(),
            P(),
            P(),
            P(),
            P(),
            P(),
            P(),
            P(),
            P(),
            P(),
            P(),
            P(),
        ),
        out_specs=(P(), P(), P(), P(), P(), P(), P(), P(), P(), P(), P(), P(), P(), P()),
        check_vma=False,
    )
```

profile of v0, /device:TPU:0, one launch (start us, length us, event | category | flops | bytes accessed | tf_op | source)
XLA Modules:
  0.0 928.3 jit_solution(7084236151416413312)
XLA Ops:
  8.8 17.7 %gather_fusion = bf16[1024,1024]{1,0:T(8,128)(2,1)} fusion(bf16[12576,1024]{1,0:T(8,128)(2,1)} %param.34, s32[1024]{0:T(1024)S(1)} %broadcast_clamp_fusion), kind=kCustom, calls=%fused_computation | custom fusion | bytes 4198400 | tf_op jit(solution)/shard_map/jit(_take)/gather | solution.py:186
  26.5 3.2 select_convert_fusion
  30.0 54.0 %all-reduce.9.cloned.1.call-done = bf16[1024,1024]{1,0:T(8,128)(2,1)} async-done(((bf16[1024,1024]{1,0:T(8,128)(2,1)}), bf16[1024,1024]{1,0:T(8,128)(2,1)}) %all-reduce.9.cloned.1.call-update) | async-done | bytes 2097168 | tf_op jit(solution)/shard_map/psum | solution.py:192
  84.0 3.0 fusion.71
  92.1 4.5 fusion.72
  96.7 26.8 %while.55 = (s32[]{:T(128)}, bf16[2,512,4,64]{1,3,2,0:T(8,128)(2,1)}, f32[2,4,512]{2,1,0:T(4,128)S(1)}, s32[2]{0:T(128)S(1)}, bf16[1,1024,3,4,64]{1,4,3,2,0:T(8,...) while((s32[]{:T(128)}, bf16[2,512,4,64]{1,3,2,0:T(8,128)(2,1)}, ...), condition=%wide.region_6.7_spmd, body=%wide.region_3.6_spmd.sunk | while | flops 562690560 | bytes 29954840 | solution.py:95
  100.7 2.7 fusion.206
  103.4 2.3 fusion.207
  105.8 4.3 fusion.208
  114.1 2.7 fusion.206
  116.8 2.3 fusion.207
  119.2 4.3 fusion.208
  125.2 2.7 fusion.123
  128.2 11.2 %psum.107 = f32[1024,4]{0,1:T(4,128)S(1)} all-reduce(f32[1024,4]{0,1:T(4,128)S(1)} %fusion.103), channel_id=1, replica_groups=mesh['batch'=8,'tensor'=4] {'tensor'}, use_global_device_ids=true, to_apply=%region_8.9 | all-reduce | flops 4096 | bytes 32768 | tf_op jit(solution)/shard_map/psum | solution.py:229
  139.4 74.4 %all-reduce.11.cloned.1.call-done = f32[1024,1024]{1,0:T(8,128)} async-done(((f32[1024,1024]{1,0:T(8,128)}), f32[1024,1024]{1,0:T(8,128)}) %all-reduce.11.cloned.1.call-update) | async-done | bytes 4194320 | tf_op jit(solution)/shard_map/psum | solution.py:229
  213.8 6.6 fusion.120
  223.6 2.4 fusion.124
  225.9 7.1 multiply_convert_fusion.2
  234.5 4.3 fusion.125
  239.5 11.4 %psum.112 = s32[4]{0:T(128)S(1)} all-reduce(s32[4]{0:T(128)S(1)} %compare_select_fusion.3), channel_id=1, replica_groups=mesh['batch'=8,'tensor'=4] {'batch'}, use_global_device_ids=true, to_apply=%region_24.25 | all-reduce | flops 4 | bytes 32 | tf_op jit(solution)/shard_map/psum | solution.py:195
  252.2 2.2 fusion.109
  254.4 12.0 %psum.109 = f32[1024,4]{0,1:T(4,128)S(1)} all-reduce(f32[1024,4]{0,1:T(4,128)S(1)} %fusion.109), channel_id=1, replica_groups=mesh['batch'=8,'tensor'=4] {'tensor'}, use_global_device_ids=true, to_apply=%region_12.13 | all-reduce | flops 4096 | bytes 32768 | tf_op jit(solution)/shard_map/psum | solution.py:249
  266.4 58.4 %all-reduce.13.cloned.1.call-done = f32[1024,1024]{1,0:T(8,128)} async-done(((f32[1024,1024]{1,0:T(8,128)}), f32[1024,1024]{1,0:T(8,128)}) %all-reduce.13.cloned.1.call-update) | async-done | bytes 4194320 | tf_op jit(solution)/shard_map/psum | solution.py:249
  324.8 6.4 fusion.121
  331.9 2.1 add_convert_fusion.1
  334.0 73.3 %while.57 = (s32[]{:T(128)}, f32[2,512]{1,0:T(2,128)S(1)}, f32[2,512]{1,0:T(2,128)S(1)}, f32[2,512]{1,0:T(2,128)S(1)}, s32[2]{0:T(128)S(1)}, /*index=5*/bf16[102...) while((s32[]{:T(128)}, f32[2,512]{1,0:T(2,128)S(1)}, ...), condition=%wide.region_19.20_spmd.clone, body=%wide.region_15.19_spmd.clone.sunk | while | flops 13225524224 | bytes 78342328 | solution.py:275
  335.3 23.4 %fusion.220 = (f32[512]{0:T(512)S(1)}, f32[512,12576]{0,1:T(8,128)}) fusion(bf16[12576,1024]{1,0:T(8,128)(2,1)} %get-tuple-element.687, bf16[1024,1024]{1,0:T(8,128)(2,1)} %get-tuple-element.686, s32[]{:T(128)S(6)} %select_n.247), kind=kOutput, calls=%fused_computation.211.clone.1 | convolution fusion | flops 13193330688 | bytes 52561924 | tf_op jit(solution)/shard_map/while/body/eval_jaxpr/dot_general | solution.py:48
  358.7 11.8 %select_reduce_fusion.2 = (f32[512]{0:T(512)S(1)}, f32[512]{0:T(512)S(1)}) fusion(f32[512,12576]{0,1:T(8,128)} %get-tuple-element.616, s32[512]{0:T(512)S(1)} %dynamic_slice.180, f32[512]{0:T(512)S(1)} %get-tuple-element.615), kind=kLoop, calls=%fused_computation.64.clone.1 | loop fusion | flops 32193536 | bytes 25763840 | tf_op jit(solution)/shard_map/while/body/eval_jaxpr/reduce_sum | solution.py:273
  371.9 23.5 %fusion.220 = (f32[512]{0:T(512)S(1)}, f32[512,12576]{0,1:T(8,128)}) fusion(bf16[12576,1024]{1,0:T(8,128)(2,1)} %get-tuple-element.687, bf16[1024,1024]{1,0:T(8,128)(2,1)} %get-tuple-element.686, s32[]{:T(128)S(6)} %select_n.247), kind=kOutput, calls=%fused_computation.211.clone.1 | convolution fusion | flops 13193330688 | bytes 52561924 | tf_op jit(solution)/shard_map/while/body/eval_jaxpr/dot_general | solution.py:48
  395.4 11.8 %select_reduce_fusion.2 = (f32[512]{0:T(512)S(1)}, f32[512]{0:T(512)S(1)}) fusion(f32[512,12576]{0,1:T(8,128)} %get-tuple-element.616, s32[512]{0:T(512)S(1)} %dynamic_slice.180, f32[512]{0:T(512)S(1)} %get-tuple-element.615), kind=kLoop, calls=%fused_computation.64.clone.1 | loop fusion | flops 32193536 | bytes 25763840 | tf_op jit(solution)/shard_map/while/body/eval_jaxpr/reduce_sum | solution.py:273
  407.4 5.9 pmax.7
  413.3 6.2 all-reduce.1
  420.1 93.1 %while.58 = (s32[]{:T(128)}, f32[2,512,1024]{2,1,0:T(8,128)}, s32[2]{0:T(128)S(1)}, f32[1024]{0:T(1024)S(1)}, bf16[1024,1024]{1,0:T(8,128)(2,1)}, /*index=5*/bf1...) while((s32[]{:T(128)}, f32[2,512,1024]{2,1,0:T(8,128)}, ...), condition=%wide.region_28.29_spmd.clone, body=%wide.region_27.28_spmd.clone.sunk | while | flops 26412417024 | bytes 80530112 | solution.py:297
  421.5 23.3 %multiply_convert_fusion.1.clone.8 = bf16[512,12576]{1,0:T(8,128)(2,1)} fusion(bf16[12576,1024]{1,0:T(8,128)(2,1)} %get-tuple-element.722, s32[512]{0:T(512)S(1)} %dynamic_slice.183, f32[512]{0:T(512)S(1)} %dynamic_slice.184, f32[512]{0:T(512)S(1)} %dynamic_slice.185, bf16[1024,1024]{1,0:T(8,128)(2,1)} %get-tuple-element.721, ...), kind=kOutput, calls=%fused_computation.70.clone.clone.clone.clone.clone.1.clone.1 | convolution fusion | flops 13225525248 | bytes 39688196 | tf_op jit(solution)/shard_map/while/body/eval_jaxpr/dot_general | solution.py:48
  444.8 21.8 %bitcast_dynamic-update-slice_fusion.5 = f32[2,512,1024]{2,1,0:T(8,128)} fusion(f32[2,512,1024]{2,1,0:T(8,128)} %get-tuple-element.706, s32[]{:T(128)} %get-tuple-element.705, bf16[12576,1024]{1,0:T(8,128)(2,1)} %get-tuple-element.722, bf16[512,12576]{1,0:T(8,128)(2,1)} %multiply_convert_fusion.1.clone.8), kind=kOutput, calls=%fused_computation.77.clone.2 | convolution fusion | flops 13186891776 | bytes 40829440 | tf_op jit(solution)/shard_map/while/body/eval_jaxpr/dot_general | solution.py:44
  468.0 23.3 %multiply_convert_fusion.1.clone.8 = bf16[512,12576]{1,0:T(8,128)(2,1)} fusion(bf16[12576,1024]{1,0:T(8,128)(2,1)} %get-tuple-element.722, s32[512]{0:T(512)S(1)} %dynamic_slice.183, f32[512]{0:T(512)S(1)} %dynamic_slice.184, f32[512]{0:T(512)S(1)} %dynamic_slice.185, bf16[1024,1024]{1,0:T(8,128)(2,1)} %get-tuple-element.721, ...), kind=kOutput, calls=%fused_computation.70.clone.clone.clone.clone.clone.1.clone.1 | convolution fusion | flops 13225525248 | bytes 39688196 | tf_op jit(solution)/shard_map/while/body/eval_jaxpr/dot_general | solution.py:48
  491.3 21.8 %bitcast_dynamic-update-slice_fusion.5 = f32[2,512,1024]{2,1,0:T(8,128)} fusion(f32[2,512,1024]{2,1,0:T(8,128)} %get-tuple-element.706, s32[]{:T(128)} %get-tuple-element.705, bf16[12576,1024]{1,0:T(8,128)(2,1)} %get-tuple-element.722, bf16[512,12576]{1,0:T(8,128)(2,1)} %multiply_convert_fusion.1.clone.8), kind=kOutput, calls=%fused_computation.77.clone.2 | convolution fusion | flops 13186891776 | bytes 40829440 | tf_op jit(solution)/shard_map/while/body/eval_jaxpr/dot_general | solution.py:44
  513.2 86.2 %all-reduce.15.cloned.1.call-done = f32[1024,1024]{1,0:T(8,128)} async-done(((f32[1024,1024]{1,0:T(8,128)}), f32[1024,1024]{1,0:T(8,128)}) %all-reduce.15.cloned.1.call-update) | async-done | bytes 4194320 | tf_op jit(solution)/shard_map/psum | solution.py:182
  599.5 4.4 multiply_reduce_fusion.2
  605.4 1.9 fusion.116
  607.7 2.4 fusion.126
  612.0 6.2 fusion.68
  618.3 2.4 fusion.127
  620.7 2.4 convolution_multiply_fusion.7
  623.2 4.7 convolution_add_fusion
  628.6 3.3 fusion.77
  631.9 3.1 convolution_bitcast_fusion.1
  638.8 74.9 %all-reduce.17.cloned.1.call-done = f32[1024,1024]{1,0:T(8,128)} async-done(((f32[1024,1024]{1,0:T(8,128)}), f32[1024,1024]{1,0:T(8,128)}) %all-reduce.17.cloned.1.call-update) | async-done | bytes 4194320 | tf_op jit(solution)/shard_map/psum | solution.py:182
  713.7 4.4 multiply_reduce_fusion.1
  726.9 2.1 fusion.74
  729.0 2.0 broadcast_in_dim.208
  731.0 34.6 %while.56 = (s32[]{:T(128)}, f32[1,1024,3,4,64]{1,4,3,2,0:T(8,128)}, bf16[1,1024,3,4,64]{1,4,3,2,0:T(8,128)(2,1)}, f32[2,4,512]{2,1,0:T(4,128)}, bf16[1,1024,4,6...) while((s32[]{:T(128)}, f32[1,1024,3,4,64]{1,4,3,2,0:T(8,128)}, ...), condition=%wide.region_37.38_spmd, body=%wide.region_35.37_spmd.sunk | while | flops 1376647680 | bytes 104919384 | solution.py:138
  732.5 2.5 fusion.215
  736.1 3.2 multiply_reduce_fusion.11
  739.3 2.4 multiply_convert_fusion.4
  744.2 2.4 fusion.216
  749.6 2.5 fusion.215
  753.2 3.2 multiply_reduce_fusion.11
  756.3 2.4 multiply_convert_fusion.4
  761.2 2.4 fusion.216
  765.8 3.7 fusion.75
  769.6 3.6 fusion.79
  776.7 39.5 %psum.113 = f32[]{:T(128)} all-reduce(f32[]{:T(128)S(6)} %select_n.168), channel_id=1, replica_groups=mesh['batch'=8,'tensor'=4] {'batch','tensor'}, use_global_device_ids=true, to_apply=%region_26.27 | all-reduce | flops 1 | bytes 8 | tf_op jit(solution)/shard_map/psum | solution.py:383
  816.2 88.6 %all-reduce.19.cloned.1.call-done = (f32[5,1024,4]{1,2,0:T(4,128)}, f32[4096,4]{0,1:T(4,128)}, f32[5,4,1024]{2,1,0:T(4,128)}, f32[4,4096]{1,0:T(4,128)}) async-done(((f32[5,1024,4]{1,2,0:T(4,128)}, f32[4096,4]{0,1:T(4,128)}, f32[5,4,1024]{2,1,0:T(4,128)}, f32[4,4096]{1,0:T(4,128)}), (f32[5,1024,4]{1,2,0:T(4,128)}, f32[4096,4]{0,1:T(4,128)}, f32[5,4,1024]{2,1,0:T(4,128)}, ...) | async-done | bytes 294928 | tf_op jit(solution)/shard_map/psum | solution.py:383
  (302 shorter events, 67.9 us)
Async XLA Ops:
  7.2 227.3 %copy-start = (bf16[1024,1024]{1,0:T(8,128)(2,1)S(1)}, bf16[1024,1024]{1,0:T(8,128)(2,1)}, u32[]{:S(2)}) copy-start(bf16[1024,1024]{1,0:T(8,128)(2,1)} %param.41) | copy-start | bytes 6291460
  7.2 76.8 %all-reduce.9.cloned.1.call-start = ((), (), s32[]{:S(2)}) async-start(), calls=%async_computation | async-start | bytes 4194304 | tf_op jit(solution)/shard_map/psum | solution.py:192
  26.5 3.3 copy-start.30
  26.5 3.4 copy-start.28
  26.5 3.4 copy-start.75
  26.5 3.4 copy-start.76
  29.8 184.0 %all-reduce.11.cloned.1.call-start = ((), (), s32[]{:S(2)}) async-start(), calls=%async_computation.1 | async-start | bytes 8388608 | tf_op jit(solution)/shard_map/psum | solution.py:229
  29.9 191.9 %copy-start.41 = (bf16[5,1024,4]{1,2,0:T(4,128)(2,1)}, bf16[5,1024,4]{1,2,0:T(4,128)(2,1)S(1)}, u32[]{:S(2)}) copy-start(bf16[5,1024,4]{1,2,0:T(4,128)(2,1)S(1)} %convert_element_type.95) | copy-start | bytes 122884
  29.9 62.2 %copy-start.40 = (f32[3,4,1024]{2,1,0:T(4,128)}, f32[3,4,1024]{2,1,0:T(4,128)S(1)}, u32[]{:S(2)}) copy-start(f32[3,4,1024]{2,1,0:T(4,128)S(1)} %slice.122) | copy-start | bytes 147460
  30.0 191.1 %copy-start.55 = (f32[1,1024]{1,0:T(1,128)}, f32[1,1024]{1,0:T(1,128)S(1)}, u32[]{:S(2)}) copy-start(f32[1,1024]{1,0:T(1,128)S(1)} %get-tuple-element.441) | copy-start | bytes 12292
  30.0 301.9 %copy-start.57 = (f32[1,1024]{1,0:T(1,128)}, f32[1,1024]{1,0:T(1,128)S(1)}, u32[]{:S(2)}) copy-start(f32[1,1024]{1,0:T(1,128)S(1)} %get-tuple-element.439) | copy-start | bytes 12292
  84.0 3.0 copy-start.10
  84.0 3.5 copy-start.11
  96.7 28.5 %copy-start.26 = (bf16[256,1024]{1,0:T(8,128)(2,1)S(1)}, bf16[256,1024]{1,0:T(8,128)(2,1)}, u32[]{:S(2)}) copy-start(bf16[256,1024]{1,0:T(8,128)(2,1)} %param.39) | copy-start | bytes 1572868
  123.5 4.4 copy-start.43
  127.9 196.9 %all-reduce.13.cloned.1.call-start = ((), (), s32[]{:S(2)}) async-start(), calls=%async_computation.2 | async-start | bytes 8388608 | tf_op jit(solution)/shard_map/psum | solution.py:249
  128.0 92.4 %copy-start.74 = (bf16[1,1024,4]{1,2,0:T(4,128)(2,1)}, bf16[1,1024,4]{1,2,0:T(4,128)(2,1)S(1)}, u32[]{:S(2)}) copy-start(bf16[1,1024,4]{1,2,0:T(4,128)(2,1)S(1)} %slice.144) | copy-start | bytes 24580
  139.4 81.0 %copy-start.36 = (f32[1024,4]{0,1:T(4,128)}, f32[1024,4]{0,1:T(4,128)S(1)}, u32[]{:S(2)}) copy-start(f32[1024,4]{0,1:T(4,128)S(1)} %psum.107) | copy-start | bytes 49156
  222.5 3.4 copy-start.12
  238.8 13.4 %copy-start.77 = (s32[1,1024]{1,0:T(1,128)S(1)}, s32[1,1024]{1,0:T(1,128)}, u32[]{:S(2)}) copy-start(s32[1,1024]{1,0:T(1,128)} %param.32) | copy-start | bytes 12292
  238.8 360.7 %all-reduce.15.cloned.1.call-start = ((), (), s32[]{:S(2)}) async-start(), calls=%async_computation.3 | async-start | bytes 8388608 | tf_op jit(solution)/shard_map/psum | solution.py:182
  266.4 64.9 %copy-start.38 = (f32[1024,4]{0,1:T(4,128)}, f32[1024,4]{0,1:T(4,128)S(1)}, u32[]{:S(2)}) copy-start(f32[1024,4]{0,1:T(4,128)S(1)} %psum.109) | copy-start | bytes 49156
  513.1 86.4 %copy-start.47 = (f32[1024]{0:T(1024)S(1)}, f32[1024]{0:T(1024)}, u32[]{:S(2)}) copy-start(f32[1024]{0:T(1024)} %copy-done.46) | copy-start | bytes 12292
  513.1 86.4 %copy-start.58 = (f32[1,1024]{1,0:T(1,128)S(1)}, f32[1,1024]{1,0:T(1,128)}, u32[]{:S(2)}) copy-start(f32[1,1024]{1,0:T(1,128)} %copy-done.57) | copy-start | bytes 12292
  513.2 90.7 %copy-start.73 = (f32[1024]{0:T(1024)S(1)}, f32[1024]{0:T(1024)}, u32[]{:S(2)}) copy-start(f32[1024]{0:T(1024)} %copy-done.72) | copy-start | bytes 12292
  513.2 90.7 %copy-start.69 = (f32[1024]{0:T(1024)S(1)}, f32[1024]{0:T(1024)}, u32[]{:S(2)}) copy-start(f32[1024]{0:T(1024)} %copy-done.68) | copy-start | bytes 12292
  513.2 200.5 %all-reduce.17.cloned.1.call-start = ((), (), s32[]{:S(2)}) async-start(), calls=%async_computation.4 | async-start | bytes 8388608 | tf_op jit(solution)/shard_map/psum | solution.py:182
  599.5 4.6 copy-start.7
  599.5 5.9 copy-start.15
  607.7 4.4 copy-start.81
  612.0 6.3 copy-start.79
  627.9 7.2 copy-start.54
  627.9 276.9 %all-reduce.19.cloned.1.call-start = ((), (), s32[]{:S(2)}) async-start(), calls=%async_computation.5 | async-start | bytes 589824 | tf_op jit(solution)/shard_map/psum | solution.py:383
  628.6 6.5 copy-start.23
  628.6 8.7 copy-start.21
  628.6 85.1 %copy-start.45 = (f32[1024]{0:T(1024)S(1)}, f32[1024]{0:T(1024)}, u32[]{:S(2)}) copy-start(f32[1024]{0:T(1024)} %copy-done.44) | copy-start | bytes 12292
  628.6 85.1 %copy-start.56 = (f32[1,1024]{1,0:T(1,128)S(1)}, f32[1,1024]{1,0:T(1,128)}, u32[]{:S(2)}) copy-start(f32[1,1024]{1,0:T(1,128)} %copy-done.55) | copy-start | bytes 12292
  638.8 79.3 %copy-start.71 = (f32[1024]{0:T(1024)S(1)}, f32[1024]{0:T(1024)}, u32[]{:S(2)}) copy-start(f32[1024]{0:T(1024)} %copy-done.70) | copy-start | bytes 12292
  638.8 79.3 %copy-start.67 = (f32[1024]{0:T(1024)S(1)}, f32[1024]{0:T(1024)}, u32[]{:S(2)}) copy-start(f32[1024]{0:T(1024)} %copy-done.66) | copy-start | bytes 12292
  713.7 4.6 copy-start.5
  713.7 5.9 copy-start.14
  725.3 3.7 copy-start.34
  732.5 3.6 copy-start.1
  732.5 3.6 copy-start.24
  749.6 3.6 copy-start.1
  749.6 3.6 copy-start.24
  765.7 3.8 copy-start.3
  765.7 7.5 copy-start.19
  765.7 8.5 copy-start.17
  765.7 8.5 copy-start.35
  765.7 9.0 copy-start.60
  765.7 9.0 copy-start.61
  765.8 9.6 %copy-start.59 = (f32[1,1024,4]{1,2,0:T(4,128)S(1)}, f32[1,1024,4]{1,2,0:T(4,128)}, u32[]{:S(2)}) copy-start(f32[1,1024,4]{1,2,0:T(4,128)} %convolution_bitcast_fusion.1) | copy-start | bytes 49156
  769.4 144.1 %copy-start.42 = (f32[4,4096]{1,0:T(4,128)S(1)}, f32[4,4096]{1,0:T(4,128)}, u32[]{:S(2)}) copy-start(f32[4,4096]{1,0:T(4,128)} %param.45) | copy-start | bytes 196612
  769.4 144.1 %copy-start.62 = (f32[4,4096]{1,0:T(4,128)S(1)}, f32[4,4096]{1,0:T(4,128)}, u32[]{:S(2)}) copy-start(f32[4,4096]{1,0:T(4,128)} %param.49) | copy-start | bytes 196612
  769.4 144.1 %copy-start.63 = (f32[4,4096]{1,0:T(4,128)S(1)}, f32[4,4096]{1,0:T(4,128)}, u32[]{:S(2)}) copy-start(f32[4,4096]{1,0:T(4,128)} %param.53) | copy-start | bytes 196612
  769.4 145.7 %copy-start.49 = (f32[5,4,1024]{2,1,0:T(4,128)S(1)}, f32[5,4,1024]{2,1,0:T(4,128)}, u32[]{:S(2)}) copy-start(f32[5,4,1024]{2,1,0:T(4,128)} %param.48) | copy-start | bytes 245764
  769.4 145.7 %copy-start.50 = (f32[5,4,1024]{2,1,0:T(4,128)S(1)}, f32[5,4,1024]{2,1,0:T(4,128)}, u32[]{:S(2)}) copy-start(f32[5,4,1024]{2,1,0:T(4,128)} %param.52) | copy-start | bytes 245764
  769.5 147.4 %copy-start.48 = (f32[4096,4]{0,1:T(4,128)S(1)}, f32[4096,4]{0,1:T(4,128)}, u32[]{:S(2)}) copy-start(f32[4096,4]{0,1:T(4,128)} %param.43) | copy-start | bytes 196612
  769.5 147.4 %copy-start.64 = (f32[4096,4]{0,1:T(4,128)S(1)}, f32[4096,4]{0,1:T(4,128)}, u32[]{:S(2)}) copy-start(f32[4096,4]{0,1:T(4,128)} %param.47) | copy-start | bytes 196612
  769.5 147.4 %copy-start.65 = (f32[4096,4]{0,1:T(4,128)S(1)}, f32[4096,4]{0,1:T(4,128)}, u32[]{:S(2)}) copy-start(f32[4096,4]{0,1:T(4,128)} %param.51) | copy-start | bytes 196612
  769.5 148.9 %copy-start.31 = (f32[5,1024,4]{1,2,0:T(4,128)S(1)}, f32[5,1024,4]{1,2,0:T(4,128)}, u32[]{:S(2)}) copy-start(f32[5,1024,4]{1,2,0:T(4,128)} %param.42) | copy-start | bytes 245764
  769.5 148.9 %copy-start.51 = (f32[5,1024,4]{1,2,0:T(4,128)S(1)}, f32[5,1024,4]{1,2,0:T(4,128)}, u32[]{:S(2)}) copy-start(f32[5,1024,4]{1,2,0:T(4,128)} %param.46) | copy-start | bytes 245764
  769.5 148.9 %copy-start.52 = (f32[5,1024,4]{1,2,0:T(4,128)S(1)}, f32[5,1024,4]{1,2,0:T(4,128)}, u32[]{:S(2)}) copy-start(f32[5,1024,4]{1,2,0:T(4,128)} %param.50) | copy-start | bytes 245764
  (28 other events, 57.8 us)
Sparse Core Ops, SparseCore 0:
  29.9 54.1 all-reduce.8
  128.1 85.6 all-reduce.10
  238.9 85.8 all-reduce.12
  513.3 86.1 all-reduce.14
  628.0 85.6 all-reduce.16
  776.2 128.5 all-reduce.18
where the time goes:
time: 938 us; the launch traced here: 928 us
  waiting for transfers between devices  437 us (47%)
  matrix products  255 us (27%)
  blocking collectives  86.1 us (9%)
  other arithmetic  80.4 us (9%)
  local copies, waits for them, and re-layouts  41.2 us (4%)
  between operations  21.2 us (2%)
    psum x2, waiting for transfers between devices, narrow_gradients(): return lax.psum(rows, 'tensor')  161 us
    dot_general x7, matrix products, plain_transposed(): lax.dot_general(left, right, (((1,), (1,)), ((), ())), preferred_element_...  98.9 us
    psum x1, waiting for transfers between devices, shards(): lax.psum((grad_a_model, grad_a_hidden, grad_b_model, grad_b_hidden, loss_...  88.6 us
    psum x1, waiting for transfers between devices, shards(): lax.psum((plain_product(attention_output, attention_output_weight), plain...  74.4 us
    psum x1, waiting for transfers between devices, shards(): lax.psum((plain_product(activation, contract_weight), plain_product(activ...  58.4 us
    dot_general x8, matrix products, plain_product(): return jnp.dot(left, right, preferred_element_type=jnp.float32)  56.1 us
    psum x1, waiting for transfers between devices, shards(): lax.psum(looked.astype(jnp.bfloat16), 'tensor').astype(jnp.float32)  54 us
    dot_general x15, matrix products, precise_product(): jnp.dot(left, right, precision=highest_accuracy, preferred_element_type=j...  50.1 us
  transfers between devices with their start and end apart: 6, of which 6 were waited for; matrix products, arithmetic and copies ran while one was open for 1% of the time, Pallas kernels for 0%

commit v1 on v0

v1 whole, which is shorter than its diff:
```python
import functools

import jax
import jax.numpy as jnp
from jax import lax
from jax.experimental import pallas as pl
from jax.experimental.pallas import tpu as pltpu
from jax.sharding import PartitionSpec as P

HEAD_DIM = 64
GROUPS = 4
ADAM_STEP = 5

beta_one = 0.9
beta_two = 0.999
learn_rate = 0.01
decay_rate = 0.01
adam_eps = 1e-08
clip_limit = 0.001
adapter_scale = 8.0
score_scale = HEAD_DIM**-0.5

CHUNKS = 2
VOCAB_BLOCK = 1536

f32 = jnp.float32
bf16 = jnp.bfloat16
NT = (((1,), (1,)), ((), ()))
TN = (((0,), (0,)), ((), ()))
VM = pl.BlockSpec(memory_space=pltpu.VMEM)
SM = pl.BlockSpec(memory_space=pltpu.SMEM)
HBM = pl.BlockSpec(memory_space=pl.ANY)


def mm(left, right):
    return jnp.dot(left, right, preferred_element_type=f32)


def mm_nt(left, right):
    return lax.dot_general(left, right, NT, preferred_element_type=f32)


def mm_tn(left, right):
    return lax.dot_general(left, right, TN, preferred_element_type=f32)


def call(kernel, outs, ins, specs, scratch=(), flops=0, name=None):
    size = sum(x.size * x.dtype.itemsize for x in ins) + sum(
        x.size * jnp.dtype(x.dtype).itemsize for x in outs
    )
    return pl.pallas_call(
        kernel,
        out_shape=tuple(outs),
        in_specs=specs,
        out_specs=tuple(VM for _ in outs),
        scratch_shapes=list(scratch),
        compiler_params=pltpu.CompilerParams(vmem_limit_bytes=56 << 20),
        cost_estimate=pl.CostEstimate(flops=int(flops), bytes_accessed=size, transcendentals=0),
        name=name,
    )(*ins)


def shape(dims, dtype):
    return jax.ShapeDtypeStruct(tuple(dims), dtype)


def split_columns(values, width):
    high = values.astype(bf16)
    column = lax.broadcasted_iota(jnp.int32, values.shape, 1)
    low = (values - high.astype(f32)).astype(bf16)
    return jnp.where((column >= width) & (column < 2 * width), low, high)


def norm_parts(values):
    centre = jnp.mean(values, -1, keepdims=True)
    centred = values - centre
    spread = jnp.mean(centred * centred, -1, keepdims=True)
    return centred, lax.rsqrt(spread + 1e-05)


def norm_kernel(place, sum_ref, got_ref, x_ref, gain_ref, shift_ref, x_out, h_out):
    values = x_ref[...].astype(f32) + (sum_ref[...].astype(f32) + got_ref[...].astype(f32))
    x_out[...] = values
    centred, inverse = norm_parts(values)
    gain = gain_ref[place : place + 1, :]
    shift = shift_ref[place : place + 1, :]
    h_out[...] = (centred * inverse * gain + shift).astype(bf16)


def norm_forward(place, total, got, x, gains, shifts):
    return call(
        functools.partial(norm_kernel, place),
        [shape(x.shape, f32), shape(x.shape, bf16)],
        [total, got, x, gains, shifts],
        [VM] * 5,
        name=f"norm_forward_{place}",
    )


def norm_back_kernel(place, has_rest, sum_ref, got_ref, x_ref, gain_ref, *rest):
    if has_rest:
        rest_ref, dx_out, low_out = rest
    else:
        dx_out, low_out = rest
    grad = sum_ref[...].astype(f32) + got_ref[...].astype(f32)
    centred, inverse = norm_parts(x_ref[...])
    hat = centred * inverse
    scaled = grad * gain_ref[place : place + 1, :]
    first = jnp.mean(scaled, -1, keepdims=True)
    second = jnp.mean(scaled * hat, -1, keepdims=True)
    dx = inverse * (scaled - first - hat * second)
    if has_rest:
        dx = dx + rest_ref[...]
    dx_out[...] = dx
    low_out[...] = dx.astype(bf16)


def norm_backward(place, total, got, x, gains, rest=None):
    ins = [total, got, x, gains] + ([] if rest is None else [rest])
    return call(
        functools.partial(norm_back_kernel, place, rest is not None),
        [shape(x.shape, f32), shape(x.shape, bf16)],
        ins,
        [VM] * len(ins),
        name=f"norm_backward_{place}",
    )


def qkv_kernel(side_ref, hm_ref, ho_ref, w_ref, a_ref, b_ref, qkv_out, h_out, u_out):
    side = side_ref[0]
    for h_ref, half in ((hm_ref, side), (ho_ref, 1 - side)):
        h = h_ref[...]
        u = split_columns(mm_nt(h, a_ref[...]), 12)
        h_out[half] = h
        u_out[half] = u
        for j in range(3):
            qkv_out[j, half] = (mm(h, w_ref[j]) + mm(u, b_ref[j])).astype(bf16)


def attention_kernel(
    place, heads, side_ref, wo_ref, a_ref, b_ref, *refs
):
    qkv_refs = refs[: place + 1]
    mine_ref, theirs_ref, o_out, lse_out, u_out, vt, ot = refs[place + 1 :]
    side = side_ref[0]
    _, _, half_rows, width = qkv_refs[0].shape
    rows = 2 * half_rows
    for p in range(place + 1):
        vt[:, p * rows : (p + 1) * rows] = jnp.transpose(
            qkv_refs[p][2].reshape(rows, width).astype(f32)
        ).astype(bf16)
    lane = lax.broadcasted_iota(jnp.int32, (half_rows, width), 1) // HEAD_DIM
    key = lax.broadcasted_iota(jnp.int32, (half_rows, half_rows), 0)
    query = lax.broadcasted_iota(jnp.int32, (half_rows, half_rows), 1)
    causal = key <= query
    for b in range(2):
        keys = [qkv_refs[p][1].reshape(rows, width) for p in range(place)]
        keys += [qkv_refs[place][1, i] for i in range(b + 1)]
        q = (qkv_refs[place][0, b].astype(f32) * score_scale).astype(bf16)
        for head in range(heads):
            q_head = jnp.where(lane == head, q, jnp.zeros_like(q))
            scores = [mm_nt(k, q_head) for k in keys]
            scores[-1] = jnp.where(causal, scores[-1], -1e30)
            peak = functools.reduce(
                jnp.maximum, [jnp.max(s, 0, keepdims=True) for s in scores]
            )
            raised = [jnp.exp(s - peak) for s in scores]
            total = functools.reduce(jnp.add, [jnp.sum(r, 0, keepdims=True) for r in raised])
            inverse = 1.0 / total
            part = None
            start = 0
            for r in raised:
                count = r.shape[0]
                weights = (r * inverse).astype(bf16)
                term = mm(
                    vt[head * HEAD_DIM : (head + 1) * HEAD_DIM, start : start + count], weights
                )
                part = term if part is None else part + term
                start += count
            ot[head * HEAD_DIM : (head + 1) * HEAD_DIM, :] = part
            lse_out[head : head + 1, b * half_rows : (b + 1) * half_rows] = peak + jnp.log(total)
        o = jnp.transpose(ot[...]).astype(bf16)
        u = split_columns(mm_nt(o, a_ref[...]), 4)
        o_out[b] = o
        u_out[b] = u
        part = mm(o, wo_ref[...]) + mm(u, b_ref[...])

        @pl.when(side == b)
        def _():
            mine_ref[...] = part

        @pl.when(side != b)
        def _():
            theirs_ref[...] = part.astype(bf16)


def mlp_kernel(
    hm_ref, ho_ref, we_ref, wc_ref, ae_ref, be_ref, ac_ref, bc_ref,
    mine_ref, theirs_ref, g_out, slope_out, ue_out, uc_out,
):
    for place, h_ref in ((1, ho_ref), (0, hm_ref)):
        h = h_ref[...]
        ue = split_columns(mm_nt(h, ae_ref[...]), 4)
        f = mm(h, we_ref[...]) + mm(ue, be_ref[...])
        square = f * f
        t = jnp.tanh(0.7978845608028654 * (f + 0.044715 * square * f))
        g = (0.5 * f * (1.0 + t)).astype(bf16)
        slope = 0.5 * (1.0 + t) + 0.5 * f * (1.0 - t * t) * (
            0.7978845608028654 + (3.0 * 0.044715 * 0.7978845608028654) * square
        )
        uc = split_columns(mm_nt(g, ac_ref[...]), 4)
        part = mm(g, wc_ref[...]) + mm(uc, bc_ref[...])
        g_out[place] = g
        slope_out[place] = slope
        ue_out[place] = ue
        uc_out[place] = uc
        if place:
            theirs_ref[...] = part.astype(bf16)
        else:
            mine_ref[...] = part


def head_kernel(
    block, hm_ref, ho_ref, et_ref, table, acc_ref, stat_ref, buf, tail, sems, peak, total, rows
):
    tail_rows = tail.shape[0]
    blocks = (table.shape[0] - tail_rows) // block
    half = hm_ref.shape[0]
    count = 2 * half

    def fetch(index, slot):
        start = pl.multiple_of(index * block, 16)
        return pltpu.make_async_copy(
            table.at[pl.ds(start, block)], buf.at[slot], sems.at[slot]
        )

    first = pltpu.make_async_copy(table.at[pl.ds(blocks * block, tail_rows)], tail, sems.at[2])
    first.start()
    fetch(0, 0).start()
    rows[:half] = hm_ref[...]
    rows[half:] = ho_ref[...]
    first.wait()
    s = mm_nt(rows[...], tail[...])
    m = jnp.max(s, -1, keepdims=True)
    p = jnp.exp(s - m)
    peak[...] = jnp.broadcast_to(m, (count, 128))
    total[...] = jnp.broadcast_to(jnp.sum(p, -1, keepdims=True), (count, 128))
    acc_ref[...] = mm(p.astype(bf16), tail[...])

    def body(index, _):
        slot = lax.rem(index, 2)

        @pl.when(index + 1 < blocks)
        def _():
            fetch(index + 1, 1 - slot).start()

        fetch(index, slot).wait()
        s = mm_nt(rows[...], buf[slot])
        m_old = peak[:, :1]
        m = jnp.maximum(m_old, jnp.max(s, -1, keepdims=True))
        decay = jnp.exp(m_old - m)
        p = jnp.exp(s - m)
        peak[...] = jnp.broadcast_to(m, (count, 128))
        total[...] = total[...] * decay + jnp.sum(p, -1, keepdims=True)
        acc_ref[...] = acc_ref[...] * decay + mm(p.astype(bf16), buf[slot])
        return 0

    lax.fori_loop(0, blocks, body, 0)
    column = lax.broadcasted_iota(jnp.int32, (count, 128), 1)
    picked = jnp.sum(rows[...].astype(f32) * et_ref[...].astype(f32), -1, keepdims=True)
    stats = jnp.where(column == 0, peak[...], jnp.where(column == 1, total[...], picked))
    stat_ref[...] = jnp.transpose(stats)[:8]


def head(hm, ho, target_rows, table):
    half, width = hm.shape
    vocab = table.shape[0]
    block = min(VOCAB_BLOCK, vocab)
    tail_rows = vocab % block or block
    return pl.pallas_call(
        functools.partial(head_kernel, block),
        out_shape=(shape((2 * half, width), f32), shape((8, 2 * half), f32)),
        in_specs=[VM, VM, VM, HBM],
        out_specs=(VM, VM),
        scratch_shapes=[
            pltpu.VMEM((2, block, width), bf16),
            pltpu.VMEM((tail_rows, width), bf16),
            pltpu.SemaphoreType.DMA((3,)),
            pltpu.VMEM((2 * half, 128), f32),
            pltpu.VMEM((2 * half, 128), f32),
            pltpu.VMEM((2 * half, width), bf16),
        ],
        compiler_params=pltpu.CompilerParams(vmem_limit_bytes=56 << 20),
        cost_estimate=pl.CostEstimate(
            flops=8 * half * vocab * width,
            bytes_accessed=2 * vocab * width,
            transcendentals=2 * half * vocab,
        ),
        name="vocabulary_head",
    )(hm, ho, target_rows, table)


def mlp_back_kernel(
    dm_ref, do_ref, hm_ref, ho_ref, g_ref, slope_ref, ue_ref, uc_ref, we_ref, wc_ref,
    bch_ref, bcl_ref, acx_ref, beh_ref, bel_ref, aex_ref,
    mine_ref, theirs_ref, gbc_ref, gac_ref, gbe_ref, gae_ref,
):
    for place, d_ref, h_ref in ((1, do_ref, ho_ref), (0, dm_ref, hm_ref)):
        d = d_ref[...]
        duc = split_columns(mm_nt(d, bch_ref[...]) + mm_nt(d, bcl_ref[...]), 4)
        dg = mm_nt(d, wc_ref[...]) + mm(duc, acx_ref[...])
        df = (dg * slope_ref[place]).astype(bf16)
        due = split_columns(mm_nt(df, beh_ref[...]) + mm_nt(df, bel_ref[...]), 4)
        part = mm_nt(df, we_ref[...]) + mm(due, aex_ref[...])
        gbc = mm_tn(uc_ref[place], d)
        gac = mm_tn(duc, g_ref[place])
        gbe = mm_tn(ue_ref[place], df)
        gae = mm_tn(due, h_ref[...])
        if place:
            theirs_ref[...] = part.astype(bf16)
            gbc_ref[...] = gbc
            gac_ref[...] = gac
            gbe_ref[...] = gbe
            gae_ref[...] = gae
        else:
            mine_ref[...] = part
            gbc_ref[...] += gbc
            gac_ref[...] += gac
            gbe_ref[...] += gbe
            gae_ref[...] += gae


def output_back_kernel(
    side_ref, dm_ref, do_ref, o_ref, u_ref, wo_ref, bh_ref, bl_ref, ax_ref,
    grad_out, gb_ref, ga_ref,
):
    side = side_ref[0]
    for place, d_ref in enumerate((dm_ref, do_ref)):
        half = side if place == 0 else 1 - side
        d = d_ref[...]
        du = split_columns(mm_nt(d, bh_ref[...]) + mm_nt(d, bl_ref[...]), 4)
        grad_out[half] = (mm_nt(d, wo_ref[...]) + mm(du, ax_ref[...])).astype(bf16)
        gb = mm_tn(u_ref[half], d)
        ga = mm_tn(du, o_ref[half])
        if place == 0:
            gb_ref[...] = gb
            ga_ref[...] = ga
        else:
            gb_ref[...] += gb
            ga_ref[...] += ga


def attention_back_kernel(chunks, heads, bh_ref, bl_ref, *refs):
    qkv_refs = refs[:chunks]
    grad_refs = refs[chunks : 2 * chunks]
    lse_refs = refs[2 * chunks : 3 * chunks]
    h_refs = refs[3 * chunks : 4 * chunks]
    u_refs = refs[4 * chunks : 5 * chunks]
    gb_ref, ga_ref, kt, dqt, dqkv = refs[5 * chunks :]
    _, _, half_rows, width = qkv_refs[0].shape
    rows = 2 * half_rows
    for p in range(chunks):
        kt[:, p * rows : (p + 1) * rows] = jnp.transpose(
            qkv_refs[p][1].reshape(rows, width).astype(f32) * score_scale
        ).astype(bf16)
    dqkv[1:] = jnp.zeros((2,) + dqkv.shape[1:], f32)
    lane = lax.broadcasted_iota(jnp.int32, (half_rows, width), 1) // HEAD_DIM
    key = lax.broadcasted_iota(jnp.int32, (half_rows, half_rows), 0)
    query = lax.broadcasted_iota(jnp.int32, (half_rows, half_rows), 1)
    causal = key <= query
    for place in range(chunks):
        for b in range(2):
            segments = [
                (p * rows, rows, qkv_refs[p][1].reshape(rows, width), qkv_refs[p][2].reshape(rows, width))
                for p in range(place)
            ]
            segments += [
                (place * rows + i * half_rows, half_rows, qkv_refs[place][1, i], qkv_refs[place][2, i])
                for i in range(b + 1)
            ]
            q = (qkv_refs[place][0, b].astype(f32) * score_scale).astype(bf16)
            grad = grad_refs[place][b]
            for head in range(heads):
                q_head = jnp.where(lane == head, q, jnp.zeros_like(q))
                grad_head = jnp.where(lane == head, grad, jnp.zeros_like(grad))
                lse = lse_refs[place][head : head + 1, b * half_rows : (b + 1) * half_rows]
                weights = []
                products = []
                inner = None
                for i, (start, count, k, v) in enumerate(segments):
                    s = mm_nt(k, q_head)
                    if i == len(segments) - 1:
                        s = jnp.where(causal, s, -1e30)
                    w = jnp.exp(s - lse)
                    dw = mm_nt(v, grad_head)
                    term = jnp.sum(w * dw, 0, keepdims=True)
                    inner = term if inner is None else inner + term
                    weights.append(w)
                    products.append(dw)
                part = None
                for (start, count, k, v), w, dw in zip(segments, weights, products):
                    ds = (w * (dw - inner)).astype(bf16)
                    dqkv[1, start : start + count, :] += mm(ds, q_head)
                    dqkv[2, start : start + count, :] += mm(w.astype(bf16), grad_head)
                    term = mm(kt[head * HEAD_DIM : (head + 1) * HEAD_DIM, start : start + count], ds)
                    part = term if part is None else part + term
                dqt[head * HEAD_DIM : (head + 1) * HEAD_DIM, :] = part
            start = place * rows + b * half_rows
            dqkv[0, start : start + half_rows, :] = jnp.transpose(dqt[...])
    for place in range(chunks):
        for b in range(2):
            start = place * rows + b * half_rows
            u = u_refs[place][b]
            t = None
            for j in range(3):
                d = dqkv[j, start : start + half_rows, :]
                high = d.astype(bf16)
                low = (d - high.astype(f32)).astype(bf16)
                gb = mm_tn(u, high) + mm_tn(u, low)
                if start == 0:
                    gb_ref[j] = gb
                else:
                    gb_ref[j] += gb
                term = mm_nt(high, bh_ref[j]) + mm_nt(high, bl_ref[j]) + mm_nt(low, bh_ref[j])
                t = term if t is None else t + term
            ga = mm_tn(split_columns(t, 12), h_refs[place][b])
            if start == 0:
                ga_ref[...] = ga
            else:
                ga_ref[...] += ga


def adam_kernel(*refs):
    grad_refs, weight_refs, first_refs, second_refs = (refs[4 * i : 4 * i + 4] for i in range(4))
    norm_ref = refs[16]
    outs = refs[17:]
    squares = jnp.zeros((1, 1), f32)
    for ref in grad_refs:
        value = ref[...]
        value = value * value
        while value.ndim > 2:
            value = jnp.sum(value, 0)
        squares = squares + jnp.sum(jnp.sum(value, 1, keepdims=True), 0, keepdims=True)
    norm = jnp.sqrt(squares)
    norm_ref[...] = jnp.broadcast_to(norm, norm_ref.shape)
    factor = clip_limit / jnp.maximum(norm, clip_limit)
    first_fix = 1.0 - beta_one**ADAM_STEP
    second_fix = 1.0 - beta_two**ADAM_STEP
    for place in range(4):
        value = grad_refs[place][...]
        grad = value * factor.reshape((1,) * value.ndim)
        first = beta_one * first_refs[place][...] + (1.0 - beta_one) * grad
        second = beta_two * second_refs[place][...] + (1.0 - beta_two) * grad * grad
        stride = first / first_fix / (jnp.sqrt(second / second_fix) + adam_eps)
        weight = weight_refs[place][...]
        outs[place][...] = weight - learn_rate * (stride + decay_rate * weight)
        outs[4 + place][...] = first
        outs[8 + place][...] = second


def adam(grads, weights, firsts, seconds):
    shapes = [shape(w.shape, f32) for w in weights]
    ins = [*grads, *weights, *firsts, *seconds]
    return call(
        adam_kernel, [shape((8, 128), f32)] + shapes * 3, ins, [VM] * 16, name="adam"
    )


def rounded(values):
    return lax.reduce_precision(values, 8, 7)


def high_low(values):
    high = rounded(values)
    return high.astype(bf16), (values - high).astype(bf16)


def stack_rows(parts):
    joined = jnp.concatenate(parts, 0)
    missing = -joined.shape[0] % 16
    return jnp.pad(joined, ((0, missing), (0, 0)))


def shards(
    tensor_size,
    batch_size,
    token_ids,
    targets,
    task_groups,
    embedding,
    positions,
    norm_gains,
    norm_shifts,
    w_qkv,
    attention_output_weight,
    expand_weight,
    contract_weight,
    model_down_maps,
    hidden_down_map,
    model_up_maps,
    hidden_up_map,
    model_down_first,
    hidden_down_first,
    model_up_first,
    hidden_up_first,
    model_down_second,
    hidden_down_second,
    model_up_second,
    hidden_up_second,
):
    assert token_ids.shape[0] == 1
    assert tensor_size >= 4 and tensor_size & (tensor_size - 1) == 0
    assert batch_size & (batch_size - 1) == 0
    index = lax.axis_index("tensor")
    side = index % 2
    length = token_ids.shape[1]
    vocab, width = embedding.shape
    part = attention_output_weight.shape[0]
    hidden = expand_weight.shape[1]
    rank = model_down_maps.shape[2]
    heads = part // HEAD_DIM
    half = length // (2 * CHUNKS)
    side_arg = side.astype(jnp.int32).reshape(1)
    steps = []
    bit = 1
    while bit < tensor_size:
        steps.append(bit)
        bit *= 2

    def swap(value, step, axis="tensor"):
        size = tensor_size if axis == "tensor" else batch_size
        return lax.ppermute(value, axis, [(i, i ^ step) for i in range(size)])

    def pick(value, which):
        return lax.dynamic_index_in_dim(value, which, 0, keepdims=False)

    def reduce_rows(mine, theirs):
        total = (mine.astype(f32) + swap(theirs, 1).astype(f32)).astype(bf16)
        for step in steps[1:-1]:
            total = (total.astype(f32) + swap(total, step).astype(f32)).astype(bf16)
        return total, swap(total, steps[-1])

    def lookup(ids):
        local = ids - index * vocab
        inside = (local >= 0) & (local < vocab)
        rows = jnp.take(embedding, jnp.clip(local, 0, vocab - 1), axis=0)
        return jnp.where(inside[..., None], rows, jnp.zeros_like(rows)), inside

    down = jnp.swapaxes(model_down_maps, 1, 2)
    down_low = down.astype(bf16)
    hidden_down = jnp.swapaxes(hidden_down_map, 0, 1)
    output_columns = lax.dynamic_slice_in_dim(down_low[3], index * part, part, 1)
    contract_columns = lax.dynamic_slice_in_dim(
        hidden_down, index * hidden, hidden, 1
    ).astype(bf16)
    up_attention = adapter_scale * lax.dynamic_slice_in_dim(
        model_up_maps[:3], index * part, part, 2
    )
    up_output = adapter_scale * model_up_maps[3]
    up_contract = adapter_scale * model_up_maps[4]
    up_expand = adapter_scale * lax.dynamic_slice_in_dim(hidden_up_map, index * hidden, hidden, 1)

    attention_rows = down_low[:3].reshape(3 * rank, width)
    a_attention = stack_rows([attention_rows] * 3)
    up_high, up_low = high_low(up_attention)
    zero = jnp.zeros((rank, part), bf16)

    def placed(value, j):
        return jnp.concatenate([value[j] if i == j else zero for i in range(3)], 0)

    b_attention = jnp.stack(
        [stack_rows([placed(up_high, j), placed(up_high, j), placed(up_low, j)]) for j in range(3)]
    )
    b_attention_high = jnp.stack([stack_rows([placed(up_high, j)] * 3) for j in range(3)])
    b_attention_low = jnp.stack([stack_rows([placed(up_low, j)] * 3) for j in range(3)])

    def triple(value):
        return stack_rows([value] * 3)

    def expanded(value):
        high, low = high_low(value)
        return stack_rows([high, high, low]), triple(high), triple(low)

    a_output, a_expand, a_contract = (
        triple(output_columns), triple(down_low[4]), triple(contract_columns),
    )
    b_output, b_output_high, b_output_low = expanded(up_output)
    b_contract, b_contract_high, b_contract_low = expanded(up_contract)
    b_expand, b_expand_high, b_expand_low = expanded(up_expand)
    twice_output, twice_expand, twice_contract = (
        stack_rows([value, value]) for value in (output_columns, down_low[4], contract_columns)
    )
    wide_rows = a_attention.shape[0]
    thin_rows = a_output.shape[0]

    member = (task_groups[:, None] == jnp.arange(GROUPS)[None, :]).astype(jnp.int32)
    counts = jnp.sum(member, 0) * length
    step = 1
    while step < batch_size:
        counts = counts + swap(counts, step, "batch")
        step *= 2
    seq_weight = (
        jnp.sum(jnp.where(member > 0, 1.0 / counts.astype(f32)[None, :], 0.0), 1) / GROUPS
    )[0]

    id_halves = token_ids.reshape(CHUNKS, 2, half)
    position_halves = positions.reshape(CHUNKS, 2, half, width)
    target_halves = targets.reshape(CHUNKS, 2, half)
    wqkv = jnp.transpose(w_qkv, (1, 0, 2))
    embedded = []
    for n in range(CHUNKS):
        theirs, _ = lookup(pick(id_halves[n], 1 - side))
        mine, _ = lookup(pick(id_halves[n], side))
        embedded.append(reduce_rows(mine, theirs))
    x0, qkv, h1, u1 = [], [], [], []
    for n in range(CHUNKS):
        x, h = norm_forward(
            0, *embedded[n], pick(position_halves[n], side), norm_gains, norm_shifts
        )
        x0.append(x)
        one = call(
            qkv_kernel,
            [
                shape((3, 2, half, part), bf16),
                shape((2, half, width), bf16),
                shape((2, half, wide_rows), bf16),
            ],
            [side_arg, h, swap(h, 1), wqkv, a_attention, b_attention],
            [SM] + [VM] * 5,
            flops=2 * 2 * half * width * 4 * part,
            name="qkv",
        )
        qkv.append(one[0])
        h1.append(one[1])
        u1.append(one[2])

    o, lse, uo, x1, h2 = [], [], [], [], []
    for n in range(CHUNKS):
        mine, theirs, o_n, lse_n, u_n = call(
            functools.partial(attention_kernel, n, heads),
            [
                shape((half, width), f32),
                shape((half, width), bf16),
                shape((2, half, part), bf16),
                shape((8, 2 * half), f32),
                shape((2, half, thin_rows), bf16),
            ],
            [side_arg, attention_output_weight, a_output, b_output] + qkv[: n + 1],
            [SM] + [VM] * (4 + n),
            scratch=[
                pltpu.VMEM((part, (n + 1) * 2 * half), bf16),
                pltpu.VMEM((part, half), f32),
            ],
            flops=2 * 2 * half * (2 * n + 1.5) * half * part * heads + 4 * half * part * width,
            name=f"attention_{n}",
        )
        o.append(o_n)
        lse.append(lse_n)
        uo.append(u_n)
        x, h = norm_forward(1, *reduce_rows(mine, theirs), x0[n], norm_gains, norm_shifts)
        x1.append(x)
        h2.append((h, swap(h, 1)))

    saved, x2, hf = [], [], []
    for n in range(CHUNKS):
        mine, theirs, *rest = call(
            mlp_kernel,
            [
                shape((half, width), f32),
                shape((half, width), bf16),
                shape((2, half, hidden), bf16),
                shape((2, half, hidden), f32),
                shape((2, half, thin_rows), bf16),
                shape((2, half, thin_rows), bf16),
            ],
            [
                *h2[n], expand_weight, contract_weight, a_expand, b_expand, a_contract, b_contract,
            ],
            [VM] * 8,
            flops=2 * 2 * half * width * hidden * 2,
            name="mlp",
        )
        saved.append(rest)
        x, h = norm_forward(2, *reduce_rows(mine, theirs), x1[n], norm_gains, norm_shifts)
        x2.append(x)
        hf.append((h, swap(h, 1)))

    losses = []
    dx2, dm = [], []
    for n in range(CHUNKS):
        order = jnp.stack([pick(target_halves[n], side), pick(target_halves[n], 1 - side)])
        rows, inside = lookup(order)
        acc, stats = head(*hf[n], rows.reshape(2 * half, width), embedding)
        acc = acc.reshape(2, half, width)
        peak, total, picked = stats[:3].reshape(3, 2, half)
        own_peak = peak
        for step in steps:
            other = swap(jnp.stack([peak, total, picked]), step)
            if step == 1:
                other = other[:, ::-1]
            higher = jnp.maximum(peak, other[0])
            total = total * jnp.exp(peak - higher) + other[1] * jnp.exp(other[0] - higher)
            picked = picked + other[2]
            peak = higher
        log_total = peak + jnp.log(total)
        losses.append(jnp.sum(log_total - picked))
        scale = seq_weight * jnp.exp(own_peak - log_total)
        wanted = seq_weight * jnp.exp(picked - log_total)
        coefficient = rounded(wanted - seq_weight) - wanted
        grad = scale[..., None] * acc + coefficient[..., None] * rows.astype(f32)
        dx, low = norm_backward(
            2, *reduce_rows(grad[0], grad[1].astype(bf16)), x2[n], norm_gains
        )
        dx2.append(dx)
        dm.append((low, swap(low, 1)))

    dx1, grads_mlp = [], []
    for n in range(CHUNKS):
        g, slope, ue, uc = saved[n]
        mine, theirs, *grads = call(
            mlp_back_kernel,
            [
                shape((half, width), f32),
                shape((half, width), bf16),
                shape((thin_rows, width), f32),
                shape((thin_rows, hidden), f32),
                shape((thin_rows, hidden), f32),
                shape((thin_rows, width), f32),
            ],
            [
                *dm[n], *h2[n], g, slope, ue, uc, expand_weight, contract_weight,
                b_contract_high, b_contract_low, twice_contract,
                b_expand_high, b_expand_low, twice_expand,
            ],
            [VM] * 16,
            flops=2 * 2 * half * width * hidden * 2,
            name="mlp_back",
        )
        grads_mlp.append(grads)
        _, low = norm_backward(1, *reduce_rows(mine, theirs), x1[n], norm_gains, dx2[n])
        dx1.append((low, swap(low, 1)))

    grad_o, grads_output = [], []
    for n in range(CHUNKS):
        grad_n, *grads = call(
            output_back_kernel,
            [
                shape((2, half, part), bf16),
                shape((thin_rows, width), f32),
                shape((thin_rows, part), f32),
            ],
            [
                side_arg, *dx1[n], o[n], uo[n], attention_output_weight,
                b_output_high, b_output_low, twice_output,
            ],
            [SM] + [VM] * 8,
            flops=4 * half * width * part * 2,
            name="output_back",
        )
        grad_o.append(grad_n)
        grads_output.append(grads)
    gb_attention, ga_attention = call(
        functools.partial(attention_back_kernel, CHUNKS, heads),
        [shape((3, wide_rows, part), f32), shape((wide_rows, width), f32)],
        [b_attention_high, b_attention_low, *qkv, *grad_o, *lse, *h1, *u1],
        [VM] * (2 + 5 * CHUNKS),
        scratch=[
            pltpu.VMEM((part, length), bf16),
            pltpu.VMEM((part, half), f32),
            pltpu.VMEM((3, length, part), f32),
        ],
        flops=5 * length * length * part * heads,
        name="attention_back",
    )

    def add_up(groups, place):
        values = [group[place] for group in groups]
        value = functools.reduce(jnp.add, values)
        return value[:rank] + value[rank : 2 * rank]

    gb_contract = adapter_scale * add_up(grads_mlp, 0)
    ga_contract = add_up(grads_mlp, 1)
    gb_expand = adapter_scale * add_up(grads_mlp, 2)
    ga_expand = add_up(grads_mlp, 3)
    gb_output = adapter_scale * add_up(grads_output, 0)
    ga_output = add_up(grads_output, 1)
    third = 3 * rank
    gb_rows = adapter_scale * (gb_attention[:, :third] + gb_attention[:, third : 2 * third])
    gb_parts = [gb_rows[j, rank * j : rank * (j + 1)] for j in range(3)]
    ga_rows = ga_attention[:third] + ga_attention[third : 2 * third]
    ga_parts = [ga_rows[rank * j : rank * (j + 1)] for j in range(3)]

    shared = jnp.concatenate([*ga_parts, ga_expand, gb_output, gb_contract], 1)
    bits = [(index // step) % 2 for step in steps]
    for step, bit in zip(steps, bits):
        columns = shared.shape[1] // 2
        keep = lax.dynamic_slice_in_dim(shared, bit * columns, columns, 1)
        send = lax.dynamic_slice_in_dim(shared, (1 - bit) * columns, columns, 1)
        shared = keep + swap(send, step)
    loss = seq_weight * functools.reduce(jnp.add, losses)
    loss_column = jnp.full((rank, 128), loss, f32)
    piece = shared.shape[1]
    own = jnp.concatenate([*gb_parts, ga_output, ga_contract, gb_expand], 1)
    bundle = jnp.concatenate([shared, own, loss_column], 1)
    step = 1
    while step < batch_size:
        bundle = bundle + swap(bundle, step, "batch")
        step *= 2
    loss = bundle[0, -1]
    gathered = bundle[None]
    for step, bit in reversed(list(zip(steps, bits))):
        other = swap(gathered, step)
        gathered = jnp.where(
            bit == 0,
            jnp.concatenate([gathered, other], 0),
            jnp.concatenate([other, gathered], 0),
        )
    order = []
    for place in range(tensor_size):
        slot = 0
        for i in range(len(steps)):
            slot = slot * 2 + (place >> i) % 2
        order.append(slot)
    whole_shared = jnp.concatenate([gathered[i, :, :piece] for i in range(tensor_size)], 1)
    shared_parts = [whole_shared[:, i * width : (i + 1) * width] for i in range(6)]

    def whole(start, count):
        return jnp.concatenate(
            [gathered[slot, :, piece + start : piece + start + count] for slot in order], 1
        )

    grad_down = jnp.stack([*shared_parts[:3], whole(3 * part, part), shared_parts[3]])
    grad_up = jnp.stack([*(whole(j * part, part) for j in range(3)), *shared_parts[4:]])
    grad_hidden_down = whole(4 * part, hidden)
    grad_hidden_up = whole(4 * part + hidden, hidden)

    def turned(values):
        return [
            jnp.swapaxes(values[0], 1, 2), jnp.swapaxes(values[1], 0, 1), values[2], values[3],
        ]

    weights = (model_down_maps, hidden_down_map, model_up_maps, hidden_up_map)
    firsts = (model_down_first, hidden_down_first, model_up_first, hidden_up_first)
    seconds = (model_down_second, hidden_down_second, model_up_second, hidden_up_second)
    norm, *news = adam(
        [grad_down, grad_hidden_down, grad_up, grad_hidden_up],
        turned(weights),
        turned(firsts),
        turned(seconds),
    )
    return (loss, norm[0, 0], *turned(news[:4]), *turned(news[4:8]), *turned(news[8:]))


def solution(mesh):
    none = P()
    return jax.shard_map(
        functools.partial(shards, mesh.shape["tensor"], mesh.shape["batch"]),
        mesh=mesh,
        in_specs=(
            P("batch", None),
            P("batch", None),
            P("batch"),
            P("tensor", None),
            none,
            none,
            none,
            P(None, None, "tensor"),
            P("tensor", None),
            P(None, "tensor"),
            P("tensor", None),
        )
        + (none,) * 12,
        out_specs=(none,) * 14,
        check_vma=False,
    )
```

time: 938 us -> 475 us (0.51)
  waiting for transfers between devices: 437 us -> 96.2 us
  matrix products: 255 us -> 0 us
  Pallas kernels: 0 us -> 201 us
  blocking collectives: 86.1 us -> 0 us
  local copies, waits for them, and re-layouts: 41.2 us -> 113 us
  other arithmetic: 80.4 us -> 23 us
  starting transfers between devices: 0.46 us -> 28.8 us
  between operations: 21.2 us -> 5.05 us
    psum x6 -> x0, waiting for transfers between devices: 437 us -> none  [the longest x2 161 us: narrow_gradients(): return lax.psum(rows, 'tensor')]
    dot_general x50 -> x0, matrix products: 255 us -> none  [the longest x7 98.9 us: plain_transposed(): lax.dot_general(left, right, (((1,), (1,)), ((), ())), preferred_element_...]
    pallas_call x0 -> x24, Pallas kernels: none -> 201 us  [the longest x22 123 us: call(): pl.pallas_call(kernel, out_shape=tuple(outs), in_specs=specs, out_specs=t...]
    ppermute x0 -> x44, waiting for transfers between devices: none -> 96.2 us  [swap(): return lax.ppermute(value, axis, [(i, i ^ step) for i in range(size)])]
    psum x5 -> x0, blocking collectives: 80.3 us -> none  [the longest x1 39.5 us: shards(): lax.psum((grad_a_model, grad_a_hidden, grad_b_model, grad_b_hidden, loss_...]
    gather x1 -> x6, local copies, waits for them, and re-layouts: 17.7 us -> 82.2 us  [lookup(): rows = jnp.take(embedding, jnp.clip(local, 0, vocab - 1), axis=0)]
    reduce_sum x18 -> x3, other arithmetic: 52.9 us -> 1.93 us  [the longest x2 1.32 us: shards(): losses.append(jnp.sum(log_total - picked))]
    ppermute x0 -> x44, starting transfers between devices: none -> 28.8 us  [swap(): return lax.ppermute(value, axis, [(i, i ^ step) for i in range(size)])]
  transfers between devices with their start and end apart: 6 -> 44, of which waited for: 6 -> 21; matrix products, arithmetic and copies ran while one was open for 1% -> 22% of each run, Pallas kernels for 0% -> 38%
where the time goes in v1:
time: 475 us; the launch traced here: 467 us
  Pallas kernels  201 us (42%)
  local copies, waits for them, and re-layouts  113 us (24%)
  waiting for transfers between devices  96.2 us (20%)
  starting transfers between devices  28.8 us (6%)
  other arithmetic  23 us (5%)
  between operations  5.05 us (1%)
    pallas_call x22, Pallas kernels, call(): pl.pallas_call(kernel, out_shape=tuple(outs), in_specs=specs, out_specs=t...  123 us
    ppermute x44, waiting for transfers between devices, swap(): return lax.ppermute(value, axis, [(i, i ^ step) for i in range(size)])  96.2 us
    gather x6, local copies, waits for them, and re-layouts, lookup(): rows = jnp.take(embedding, jnp.clip(local, 0, vocab - 1), axis=0)  82.2 us
    pallas_call x2, Pallas kernels, head(): pl.pallas_call(functools.partial(head_kernel, block), out_shape=(shape((2...  77.5 us
    ppermute x44, starting transfers between devices, swap(): return lax.ppermute(value, axis, [(i, i ^ step) for i in range(size)])  28.8 us
    unnamed x112, local copies, waits for them, and re-layouts  13.9 us
  transfers between devices with their start and end apart: 44, of which 21 were waited for; matrix products, arithmetic and copies ran while one was open for 22% of the time, Pallas kernels for 38%

profile of v1, /device:TPU:0, one launch (start us, length us, event | category | flops | bytes accessed | tf_op | source)
XLA Modules:
  0.0 466.5 jit_solution(6531707112903562286)
XLA Ops:
  1.6 13.2 %gather_fusion.1 = bf16[256,1024]{1,0:T(8,128)(2,1)S(1)} fusion(bf16[12576,1024]{1,0:T(8,128)(2,1)} %table.3, s32[1024]{0:T(1024)S(1)} %pad_clamp_fusion.4), kind=kCustom, calls=%fused_computation.2.clone | custom fusion | bytes 1049600 | tf_op jit(solution)/shard_map/jit(_take)/gather | solution.py:546
  15.5 13.2 %gather_fusion.3 = bf16[256,1024]{1,0:T(8,128)(2,1)S(1)} fusion(bf16[12576,1024]{1,0:T(8,128)(2,1)} %table.3, s32[1024]{0:T(1024)S(1)} %pad_clamp_fusion.2), kind=kCustom, calls=%fused_computation.4.clone | custom fusion | bytes 1049600 | tf_op jit(solution)/shard_map/jit(_take)/gather | solution.py:546
  30.7 1.7 fusion.83
  32.4 13.2 %gather_fusion = bf16[256,1024]{1,0:T(8,128)(2,1)S(1)} fusion(bf16[12576,1024]{1,0:T(8,128)(2,1)} %table.3, s32[1024]{0:T(1024)S(1)} %pad_clamp_fusion.5), kind=kCustom, calls=%fused_computation.clone | custom fusion | bytes 1049600 | tf_op jit(solution)/shard_map/jit(_take)/gather | solution.py:546
  45.6 1.3 add_convert_fusion.7.sum_ref
  46.9 3.0 collective-permute-start.1
  50.0 13.2 %gather_fusion.2 = bf16[256,1024]{1,0:T(8,128)(2,1)S(1)} fusion(bf16[12576,1024]{1,0:T(8,128)(2,1)} %table.3, s32[1024]{0:T(1024)S(1)} %pad_clamp_fusion.3), kind=kCustom, calls=%fused_computation.3.clone | custom fusion | bytes 1049600 | tf_op jit(solution)/shard_map/jit(_take)/gather | solution.py:546
  64.0 1.3 add_convert_fusion.6.sum_ref
  66.2 2.8 norm_forward_0.2
  70.6 8.4 %collective-permute-done.4.got_ref = bf16[256,1024]{1,0:T(8,128)(2,1)S(1)} collective-permute-done((bf16[256,1024]{1,0:T(8,128)(2,1)S(1)}, bf16[256,1024]{1,0:T(8,128)(2,1)S(1)}, u32[]{:S(2)}, u32[]{:S(2)}) %collective-permute-start.4) | collective-permute-done | bytes 524320 | tf_op jit(solution)/shard_map/ppermute | solution.py:532
  79.8 2.7 norm_forward_0.3
  85.3 4.9 %qkv.2 = (bf16[3,2,256,256]{3,2,1,0:T(8,128)(2,1)}, bf16[2,256,1024]{2,1,0:T(8,128)(2,1)}, bf16[2,256,48]{2,1,0:T(8,128)(2,1)}) custom-call(s32[1]{0:T(128)} %bitcast.12.side_ref, bf16[256,1024]{1,0:T(8,128)(2,1)} %get-tuple-element.99.hm_ref, bf16[256,1024]{1,0:T(8,128)(2,1)} %copy-done.49, bf16[3,1024,256]{2,1,0:T(8,128)(2,1)} %bitcast.369, ...), custom_call_target="tpu_custom_call" | custom-call | flops 1073741824 | bytes 4677636 | tf_op jit(solution)/shard_map/qkv/pallas_call | solution.py:51
  90.2 6.4 %attention_0.1 = (f32[256,1024]{1,0:T(8,128)}, bf16[256,1024]{1,0:T(8,128)(2,1)}, bf16[2,256,256]{2,1,0:T(8,128)(2,1)}, f32[8,512]{1,0:T(8,128)}, bf16[2,256,16]{2,1,0:T(8,128)(2,1)}) custom-call(s32[1]{0:T(128)} %bitcast.12.side_ref, bf16[256,1024]{1,0:T(8,128)(2,1)} %wo_ref.7, bf16[16,256]{1,0:T(8,128)(2,1)} %get-tuple-element.284.a_ref, ...), custom_call_target="tpu_custom_call" | custom-call | flops 671088640 | bytes 3219460 | tf_op jit(solution)/shard_map/attention_0/pallas_call | solution.py:51
  97.1 1.5 collective-permute-start.6
  100.2 4.5 qkv.3
  104.6 9.1 %attention_1.1 = (f32[256,1024]{1,0:T(8,128)}, bf16[256,1024]{1,0:T(8,128)(2,1)}, bf16[2,256,256]{2,1,0:T(8,128)(2,1)}, f32[8,512]{1,0:T(8,128)}, bf16[2,256,16]{2,1,0:T(8,128)(2,1)}) custom-call(s32[1]{0:T(128)} %bitcast.12.side_ref, bf16[256,1024]{1,0:T(8,128)(2,1)} %wo_ref.7, bf16[16,256]{1,0:T(8,128)(2,1)} %get-tuple-element.284.a_ref, ...), custom_call_target="tpu_custom_call" | custom-call | flops 1207959552 | bytes 4005892 | tf_op jit(solution)/shard_map/attention_1/pallas_call | solution.py:51
  117.2 1.4 collective-permute-start.24
  118.7 10.2 %collective-permute-done.10.got_ref = bf16[256,1024]{1,0:T(8,128)(2,1)S(1)} collective-permute-done((bf16[256,1024]{1,0:T(8,128)(2,1)S(1)}, bf16[256,1024]{1,0:T(8,128)(2,1)S(1)}, u32[]{:S(2)}, u32[]{:S(2)}) %collective-permute-start.10) | collective-permute-done | bytes 524320 | tf_op jit(solution)/shard_map/ppermute | solution.py:532
  129.6 2.9 norm_forward_1.2
  134.0 5.6 %collective-permute-done.24.got_ref = bf16[256,1024]{1,0:T(8,128)(2,1)S(1)} collective-permute-done((bf16[256,1024]{1,0:T(8,128)(2,1)S(1)}, bf16[256,1024]{1,0:T(8,128)(2,1)S(1)}, u32[]{:S(2)}, u32[]{:S(2)}) %collective-permute-start.24) | collective-permute-done | bytes 524320 | tf_op jit(solution)/shard_map/ppermute | solution.py:532
  140.4 2.9 norm_forward_1.3
  144.1 9.3 %mlp.2 = (f32[256,1024]{1,0:T(8,128)}, bf16[256,1024]{1,0:T(8,128)(2,1)}, bf16[2,256,1024]{2,1,0:T(8,128)(2,1)}, f32[2,256,1024]{2,1,0:T(8,128)}, bf16[2,256,16]...) custom-call(bf16[256,1024]{1,0:T(8,128)(2,1)} %get-tuple-element.106.hm_ref, bf16[256,1024]{1,0:T(8,128)(2,1)} %copy-done.17, ...), custom_call_target="tpu_custom_call" | custom-call | flops 2147483648 | bytes 10125312 | tf_op jit(solution)/shard_map/mlp/pallas_call | solution.py:51
  153.8 14.6 %gather_fusion.4 = bf16[512,1024]{1,0:T(8,128)(2,1)S(1)} fusion(bf16[12576,1024]{1,0:T(8,128)(2,1)} %table.3, s32[1024]{0:T(1024)S(1)} %pad_clamp_fusion.1), kind=kCustom, calls=%fused_computation.1.clone | custom fusion | bytes 2099200 | tf_op jit(solution)/shard_map/jit(_take)/gather | solution.py:546
  168.4 14.8 %gather_fusion.5 = bf16[512,1024]{1,0:T(8,128)(2,1)S(1)} fusion(bf16[12576,1024]{1,0:T(8,128)(2,1)} %table.3, s32[1024]{0:T(1024)S(1)} %pad_clamp_fusion), kind=kCustom, calls=%fused_computation.5.clone | custom fusion | bytes 2099200 | tf_op jit(solution)/shard_map/jit(_take)/gather | solution.py:546
  183.3 1.3 select_select_fusion.1
  184.6 9.4 %mlp.3 = (f32[256,1024]{1,0:T(8,128)}, bf16[256,1024]{1,0:T(8,128)(2,1)}, bf16[2,256,1024]{2,1,0:T(8,128)(2,1)}, f32[2,256,1024]{2,1,0:T(8,128)}, bf16[2,256,16]...) custom-call(bf16[256,1024]{1,0:T(8,128)(2,1)} %get-tuple-element.129.hm_ref, ...), custom_call_target="tpu_custom_call" | custom-call | flops 2147483648 | bytes 10125312 | tf_op jit(solution)/shard_map/mlp/pallas_call | solution.py:51
  194.0 1.3 add_convert_fusion.4.sum_ref
  195.8 1.2 select_select_fusion
  197.2 1.6 collective-permute-start.27
  198.8 11.3 %collective-permute-done.13.got_ref = bf16[256,1024]{1,0:T(8,128)(2,1)S(1)} collective-permute-done((bf16[256,1024]{1,0:T(8,128)(2,1)S(1)}, bf16[256,1024]{1,0:T(8,128)(2,1)S(1)}, u32[]{:S(2)}, u32[]{:S(2)}) %collective-permute-start.13) | collective-permute-done | bytes 524320 | tf_op jit(solution)/shard_map/ppermute | solution.py:532
  210.9 2.9 norm_forward_2.2
  213.9 1.6 collective-permute-start.7
  215.5 2.0 collective-permute-done.7
  217.5 2.6 collective-permute-start.8
  220.1 1.9 collective-permute-done.8
  224.0 2.9 norm_forward_2.3
  227.0 38.8 %vocabulary_head.2 = (f32[512,1024]{1,0:T(8,128)}, f32[8,512]{1,0:T(8,128)}) custom-call(bf16[256,1024]{1,0:T(8,128)(2,1)} %get-tuple-element.110.hm_ref, bf16[256,1024]{1,0:T(8,128)(2,1)} %collective-permute-done.14.ho_ref, bf16[512,1024]{1,0:T(8,128)(2,1)} %bitcast.343, bf16[12576,1024]{1,0:T(8,128)(2,1)} %table.3), custom_call_target="tpu_custom_call" | custom-call | flops 26373783552 | bytes 25755648 | tf_op jit(solution)/shard_map/vocabulary_head/pallas_call | solution.py:280
  268.1 38.7 %vocabulary_head.3 = (f32[512,1024]{1,0:T(8,128)}, f32[8,512]{1,0:T(8,128)}) custom-call(bf16[256,1024]{1,0:T(8,128)(2,1)} %get-tuple-element.133.hm_ref, bf16[256,1024]{1,0:T(8,128)(2,1)} %copy-done.50, bf16[512,1024]{1,0:T(8,128)(2,1)} %bitcast.344, bf16[12576,1024]{1,0:T(8,128)(2,1)} %table.3), custom_call_target="tpu_custom_call" | custom-call | flops 26373783552 | bytes 25755648 | tf_op jit(solution)/shard_map/vocabulary_head/pallas_call | solution.py:280
  309.2 1.4 collective-permute-start.30
  310.6 1.2 collective-permute-done.16
  312.5 2.2 multiply_add_fusion.1
  319.4 12.5 %collective-permute-done.18.got_ref = bf16[256,1024]{1,0:T(8,128)(2,1)S(1)} collective-permute-done((bf16[256,1024]{1,0:T(8,128)(2,1)S(1)}, bf16[256,1024]{1,0:T(8,128)(2,1)S(1)}, u32[]{:S(2)}, u32[]{:S(2)}) %collective-permute-start.18) | collective-permute-done | bytes 524320 | tf_op jit(solution)/shard_map/ppermute | solution.py:532
  332.7 3.4 norm_backward_2.2
  336.1 6.2 %collective-permute-done.32.got_ref = bf16[256,1024]{1,0:T(8,128)(2,1)S(1)} collective-permute-done((bf16[256,1024]{1,0:T(8,128)(2,1)S(1)}, bf16[256,1024]{1,0:T(8,128)(2,1)S(1)}, u32[]{:S(2)}, u32[]{:S(2)}) %collective-permute-start.32) | collective-permute-done | bytes 524320 | tf_op jit(solution)/shard_map/ppermute | solution.py:532
  343.1 3.4 norm_backward_2.3
  349.8 11.2 %mlp_back.2 = (f32[256,1024]{1,0:T(8,128)}, bf16[256,1024]{1,0:T(8,128)(2,1)}, f32[16,1024]{1,0:T(8,128)}, f32[16,1024]{1,0:T(8,128)}, f32[16,1024]{1,0:T(8,128)}, /*index=5*/f32[16,1024]{1,0:T(8,128)}) custom-call(bf16[256,1024]{1,0:T(8,128)(2,1)} %get-tuple-element.114.dm_ref, bf16[256,1024]{1,0:T(8,128)(2,1)} %copy-done.22, ...), custom_call_target="tpu_custom_call" | custom-call | flops 2147483648 | bytes 11501568 | tf_op jit(solution)/shard_map/mlp_back/pallas_call | solution.py:51
  362.4 11.2 %mlp_back.3 = (f32[256,1024]{1,0:T(8,128)}, bf16[256,1024]{1,0:T(8,128)(2,1)}, f32[16,1024]{1,0:T(8,128)}, f32[16,1024]{1,0:T(8,128)}, f32[16,1024]{1,0:T(8,128)}, /*index=5*/f32[16,1024]{1,0:T(8,128)}) custom-call(bf16[256,1024]{1,0:T(8,128)(2,1)} %get-tuple-element.137.dm_ref, bf16[256,1024]{1,0:T(8,128)(2,1)} %copy-done.20, ...), custom_call_target="tpu_custom_call" | custom-call | flops 2147483648 | bytes 11501568 | tf_op jit(solution)/shard_map/mlp_back/pallas_call | solution.py:51
  374.4 1.4 collective-permute-done.34
  377.1 11.6 %collective-permute-done.21.got_ref = bf16[256,1024]{1,0:T(8,128)(2,1)S(1)} collective-permute-done((bf16[256,1024]{1,0:T(8,128)(2,1)S(1)}, bf16[256,1024]{1,0:T(8,128)(2,1)S(1)}, u32[]{:S(2)}, u32[]{:S(2)}) %collective-permute-start.21) | collective-permute-done | bytes 524320 | tf_op jit(solution)/shard_map/ppermute | solution.py:532
  389.5 3.8 norm_backward_1.2
  393.5 6.0 %collective-permute-done.35.got_ref = bf16[256,1024]{1,0:T(8,128)(2,1)S(1)} collective-permute-done((bf16[256,1024]{1,0:T(8,128)(2,1)S(1)}, bf16[256,1024]{1,0:T(8,128)(2,1)S(1)}, u32[]{:S(2)}, u32[]{:S(2)}) %collective-permute-start.35) | collective-permute-done | bytes 524320 | tf_op jit(solution)/shard_map/ppermute | solution.py:532
  400.3 3.7 norm_backward_1.3
  408.0 4.2 output_back.2
  413.0 4.2 output_back.3
  417.2 15.0 %attention_back.1 = (f32[3,48,256]{2,1,0:T(8,128)}, f32[48,1024]{1,0:T(8,128)}) custom-call(bf16[3,48,256]{2,1,0:T(8,128)(2,1)} %pad_maximum_fusion.bh_ref, bf16[3,48,256]{2,1,0:T(8,128)(2,1)} %pad_maximum_fusion.1.bl_ref, bf16[3,2,256,256]{3,2,1,0:T(8,128)(2,1)} %get-tuple-element.100.refs_0_, bf16[3,2,256,256]{3,2,1,0:T(8,128)(2,1)} %get-tuple-element.102.refs_1_, ...), custom_call_target="tpu_custom_call" | custom-call | flops 5368709120 | bytes 4816896 | tf_op jit(solution)/shard_map/attention_back/pallas_call | solution.py:51
  437.0 2.3 collective-permute-done.38
  440.0 3.9 collective-permute-done.39
  443.8 1.6 collective-permute-start.40
  445.5 2.8 collective-permute-done.40
  448.3 3.5 collective-permute-start.41
  451.8 3.2 collective-permute-done.41
  455.5 3.9 collective-permute-done.42
  462.5 2.5 adam.1
  464.9 1.2 slice.433
  (336 shorter events, 54.5 us)
Async XLA Ops:
  14.9 30.7 %collective-permute-start = (bf16[256,1024]{1,0:T(8,128)(2,1)S(1)}, bf16[256,1024]{1,0:T(8,128)(2,1)}, u32[]{:S(2)}, u32[]{:S(2)}) collective-permute-start(bf16[256,1024]{1,0:T(8,128)(2,1)S(1)} %select_select_fusion.4), channel_id=1, source_target_pairs={{0,1},{1,0},{2,3},{3,2},{4,5},{5,4},{6,7},{7,6},{8,9},{9,8},{10,11... | collective-permute-start | bytes 1572872 | tf_op jit(solution)/shard_map/ppermute | solution.py:532
  15.5 14.3 %copy-start.31 = (f32[5,4,1024]{2,1,0:T(4,128)S(1)}, f32[5,4,1024]{2,1,0:T(4,128)}, u32[]{:S(2)}) copy-start(f32[5,4,1024]{2,1,0:T(4,128)} %refs_6_.1) | copy-start | bytes 245764
  15.5 14.3 %copy-start.32 = (f32[5,1024,4]{1,2,0:T(4,128)S(1)}, f32[5,1024,4]{1,2,0:T(4,128)}, u32[]{:S(2)}) copy-start(f32[5,1024,4]{1,2,0:T(4,128)} %param.38) | copy-start | bytes 245764
  15.5 14.3 %slice-start = ((f32[5,4,1024]{2,1,0:T(4,128)}), f32[3,4,1024]{2,1,0:T(4,128)S(1)}, s32[]{:S(2)}) async-start(f32[5,4,1024]{2,1,0:T(4,128)} %refs_6_.1), calls=%async_computation | async-start | bytes 98304 | tf_op jit(solution)/shard_map/slice | solution.py:557
  29.7 34.3 %collective-permute-start.3 = (bf16[256,1024]{1,0:T(8,128)(2,1)}, bf16[256,1024]{1,0:T(8,128)(2,1)}, u32[]{:S(2)}, u32[]{:S(2)}) collective-permute-start(bf16[256,1024]{1,0:T(8,128)(2,1)} %select_select_fusion.2), channel_id=1, source_target_pairs={{0,1},{1,0},{2,3},{3,2},{4,5},{5,4},{6,7},{7,6},{8,9},{9,8},{10,11... | collective-permute-start | bytes 1572872 | tf_op jit(solution)/shard_map/ppermute | solution.py:532
  46.9 16.3 %copy-start.2 = (bf16[256,1024]{1,0:T(8,128)(2,1)}, bf16[256,1024]{1,0:T(8,128)(2,1)S(1)}, u32[]{:S(2)}) copy-start(bf16[256,1024]{1,0:T(8,128)(2,1)S(1)} %add_convert_fusion.7.sum_ref) | copy-start | bytes 1572868
  46.9 19.3 %collective-permute-start.1 = (bf16[256,1024]{1,0:T(8,128)(2,1)S(1)}, bf16[256,1024]{1,0:T(8,128)(2,1)}, u32[]{:S(2)}, u32[]{:S(2)}) collective-permute-start(bf16[256,1024]{1,0:T(8,128)(2,1)S(1)} %add_convert_fusion.7.sum_ref), channel_id=1, source_target_pairs={{0,2},{1,3},{2,0},{3,1},{4,6},{5,7},{6,4},{7,5},{8,10},{9,11},{10,... | collective-permute-start | bytes 1572872 | tf_op jit(solution)/shard_map/ppermute | solution.py:532
  65.4 13.6 %collective-permute-start.4 = (bf16[256,1024]{1,0:T(8,128)(2,1)S(1)}, bf16[256,1024]{1,0:T(8,128)(2,1)S(1)}, u32[]{:S(2)}, u32[]{:S(2)}) collective-permute-start(bf16[256,1024]{1,0:T(8,128)(2,1)S(1)} %add_convert_fusion.6.sum_ref), channel_id=1, source_target_pairs={{0,2},{1,3},{2,0},{3,1},{4,6},{5,7},{6,4},{7,5},{8,10},{9,11},{10,... | collective-permute-start | bytes 1572872 | tf_op jit(solution)/shard_map/ppermute | solution.py:532
  69.0 15.5 %collective-permute-start.2 = (bf16[256,1024]{1,0:T(8,128)(2,1)}, bf16[256,1024]{1,0:T(8,128)(2,1)S(1)}, u32[]{:S(2)}, u32[]{:S(2)}) collective-permute-start(bf16[256,1024]{1,0:T(8,128)(2,1)} %get-tuple-element.99.hm_ref), channel_id=1, source_target_pairs={{0,1},{1,0},{2,3},{3,2},{4,5},{5,4},{6,7},{7,6},{8,9},{9,8},{10,11... | collective-permute-start | bytes 1572872 | tf_op jit(solution)/shard_map/ppermute | solution.py:532
  82.6 16.8 %collective-permute-start.5 = (bf16[256,1024]{1,0:T(8,128)(2,1)}, bf16[256,1024]{1,0:T(8,128)(2,1)S(1)}, u32[]{:S(2)}, u32[]{:S(2)}) collective-permute-start(bf16[256,1024]{1,0:T(8,128)(2,1)} %get-tuple-element.101.hm_ref), channel_id=1, source_target_pairs={{0,1},{1,0},{2,3},{3,2},{4,5},{5,4},{6,7},{7,6},{8,9},{9,8},{10,11... | collective-permute-start | bytes 1572872 | tf_op jit(solution)/shard_map/ppermute | solution.py:532
  96.6 17.2 %collective-permute-start.9 = (bf16[256,1024]{1,0:T(8,128)(2,1)}, bf16[256,1024]{1,0:T(8,128)(2,1)S(1)}, u32[]{:S(2)}, u32[]{:S(2)}) collective-permute-start(bf16[256,1024]{1,0:T(8,128)(2,1)} %get-tuple-element.104), channel_id=1, source_target_pairs={{0,1},{1,0},{2,3},{3,2},{4,5},{5,4},{6,7},{7,6},{8,9},{9,8},{10,11... | collective-permute-start | bytes 1572872 | tf_op jit(solution)/shard_map/ppermute | solution.py:532
  97.1 116.8 %collective-permute-start.6 = (s32[4]{0:T(128)S(1)}, s32[4]{0:T(128)S(1)}, u32[]{:S(2)}, u32[]{:S(2)}) collective-permute-start(s32[4]{0:T(128)S(1)} %compare_select_fusion.7), channel_id=1, source_target_pairs={{0,4},{4,0},{8,12},{12,8},{16,20},{20,16},{24,28},{28,24},{1,5},{5... | collective-permute-start | bytes 56 | tf_op jit(solution)/shard_map/ppermute | solution.py:532
  113.7 2.3 collective-permute-start.23
  114.0 14.9 %copy-start.5 = (bf16[256,1024]{1,0:T(8,128)(2,1)}, bf16[256,1024]{1,0:T(8,128)(2,1)S(1)}, u32[]{:S(2)}) copy-start(bf16[256,1024]{1,0:T(8,128)(2,1)S(1)} %add_convert_fusion.5.sum_ref) | copy-start | bytes 1572868
  114.0 14.9 %collective-permute-start.10 = (bf16[256,1024]{1,0:T(8,128)(2,1)S(1)}, bf16[256,1024]{1,0:T(8,128)(2,1)S(1)}, u32[]{:S(2)}, u32[]{:S(2)}) collective-permute-start(bf16[256,1024]{1,0:T(8,128)(2,1)S(1)} %add_convert_fusion.5.sum_ref), channel_id=1, source_target_pairs={{0,2},{1,3},{2,0},{3,1},{4,6},{5,7},{6,4},{7,5},{8,10},{9,11},{10,... | collective-permute-start | bytes 1572872 | tf_op jit(solution)/shard_map/ppermute | solution.py:532
  117.2 22.4 %copy-start.3 = (bf16[256,1024]{1,0:T(8,128)(2,1)}, bf16[256,1024]{1,0:T(8,128)(2,1)S(1)}, u32[]{:S(2)}) copy-start(bf16[256,1024]{1,0:T(8,128)(2,1)S(1)} %add_convert_fusion.2.sum_ref) | copy-start | bytes 1572868
  117.2 22.4 %collective-permute-start.24 = (bf16[256,1024]{1,0:T(8,128)(2,1)S(1)}, bf16[256,1024]{1,0:T(8,128)(2,1)S(1)}, u32[]{:S(2)}, u32[]{:S(2)}) collective-permute-start(bf16[256,1024]{1,0:T(8,128)(2,1)S(1)} %add_convert_fusion.2.sum_ref), channel_id=1, source_target_pairs={{0,2},{1,3},{2,0},{3,1},{4,6},{5,7},{6,4},{7,5},{8,10},{9,11},{10,... | collective-permute-start | bytes 1572872 | tf_op jit(solution)/shard_map/ppermute | solution.py:532
  132.5 10.8 %collective-permute-start.11 = (bf16[256,1024]{1,0:T(8,128)(2,1)}, bf16[256,1024]{1,0:T(8,128)(2,1)S(1)}, u32[]{:S(2)}, u32[]{:S(2)}) collective-permute-start(bf16[256,1024]{1,0:T(8,128)(2,1)} %get-tuple-element.106.hm_ref), channel_id=1, source_target_pairs={{0,1},{1,0},{2,3},{3,2},{4,5},{5,4},{6,7},{7,6},{8,9},{9,8},{10,11... | collective-permute-start | bytes 1572872 | tf_op jit(solution)/shard_map/ppermute | solution.py:532
  143.3 41.3 %collective-permute-start.25 = (bf16[256,1024]{1,0:T(8,128)(2,1)}, bf16[256,1024]{1,0:T(8,128)(2,1)}, u32[]{:S(2)}, u32[]{:S(2)}) collective-permute-start(bf16[256,1024]{1,0:T(8,128)(2,1)} %get-tuple-element.129.hm_ref), channel_id=1, source_target_pairs={{0,1},{1,0},{2,3},{3,2},{4,5},{5,4},{6,7},{7,6},{8,9},{9,8},{10,11... | collective-permute-start | bytes 1572872 | tf_op jit(solution)/shard_map/ppermute | solution.py:532
  153.3 40.6 %collective-permute-start.12 = (bf16[256,1024]{1,0:T(8,128)(2,1)}, bf16[256,1024]{1,0:T(8,128)(2,1)}, u32[]{:S(2)}, u32[]{:S(2)}) collective-permute-start(bf16[256,1024]{1,0:T(8,128)(2,1)} %get-tuple-element.108), channel_id=1, source_target_pairs={{0,1},{1,0},{2,3},{3,2},{4,5},{5,4},{6,7},{7,6},{8,9},{9,8},{10,11... | collective-permute-start | bytes 1572872 | tf_op jit(solution)/shard_map/ppermute | solution.py:532
  193.9 3.1 collective-permute-start.26
  195.3 14.9 %collective-permute-start.13 = (bf16[256,1024]{1,0:T(8,128)(2,1)S(1)}, bf16[256,1024]{1,0:T(8,128)(2,1)S(1)}, u32[]{:S(2)}, u32[]{:S(2)}) collective-permute-start(bf16[256,1024]{1,0:T(8,128)(2,1)S(1)} %add_convert_fusion.4.sum_ref), channel_id=1, source_target_pairs={{0,2},{1,3},{2,0},{3,1},{4,6},{5,7},{6,4},{7,5},{8,10},{9,11},{10,... | collective-permute-start | bytes 1572872 | tf_op jit(solution)/shard_map/ppermute | solution.py:532
  197.2 26.1 %copy-start.4 = (bf16[256,1024]{1,0:T(8,128)(2,1)}, bf16[256,1024]{1,0:T(8,128)(2,1)S(1)}, u32[]{:S(2)}) copy-start(bf16[256,1024]{1,0:T(8,128)(2,1)S(1)} %add_convert_fusion.1.sum_ref) | copy-start | bytes 1572868
  197.2 26.0 %collective-permute-start.27 = (bf16[256,1024]{1,0:T(8,128)(2,1)S(1)}, bf16[256,1024]{1,0:T(8,128)(2,1)S(1)}, u32[]{:S(2)}, u32[]{:S(2)}) collective-permute-start(bf16[256,1024]{1,0:T(8,128)(2,1)S(1)} %add_convert_fusion.1.sum_ref), channel_id=1, source_target_pairs={{0,2},{1,3},{2,0},{3,1},{4,6},{5,7},{6,4},{7,5},{8,10},{9,11},{10,... | collective-permute-start | bytes 1572872 | tf_op jit(solution)/shard_map/ppermute | solution.py:532
  213.8 13.1 %collective-permute-start.14 = (bf16[256,1024]{1,0:T(8,128)(2,1)}, bf16[256,1024]{1,0:T(8,128)(2,1)}, u32[]{:S(2)}, u32[]{:S(2)}) collective-permute-start(bf16[256,1024]{1,0:T(8,128)(2,1)} %get-tuple-element.110.hm_ref), channel_id=1, source_target_pairs={{0,1},{1,0},{2,3},{3,2},{4,5},{5,4},{6,7},{7,6},{8,9},{9,8},{10,11... | collective-permute-start | bytes 1572872 | tf_op jit(solution)/shard_map/ppermute | solution.py:532
  213.9 3.6 collective-permute-start.7
  217.5 4.5 collective-permute-start.8
  227.0 40.3 %collective-permute-start.28 = (bf16[256,1024]{1,0:T(8,128)(2,1)}, bf16[256,1024]{1,0:T(8,128)(2,1)S(1)}, u32[]{:S(2)}, u32[]{:S(2)}) collective-permute-start(bf16[256,1024]{1,0:T(8,128)(2,1)} %get-tuple-element.133.hm_ref), channel_id=1, source_target_pairs={{0,1},{1,0},{2,3},{3,2},{4,5},{5,4},{6,7},{7,6},{8,9},{9,8},{10,11... | collective-permute-start | bytes 1572872 | tf_op jit(solution)/shard_map/ppermute | solution.py:532
  266.7 41.2 %collective-permute-start.15 = (f32[3,2,256]{2,1,0:T(2,128)S(1)}, f32[3,2,256]{2,1,0:T(2,128)S(1)}, u32[]{:S(2)}, u32[]{:S(2)}) collective-permute-start(f32[3,2,256]{2,1,0:T(2,128)S(1)} %pad_maximum_fusion.16), channel_id=1, source_target_pairs={{0,1},{1,0},{2,3},{3,2},{4,5},{5,4},{6,7},{7,6},{8,9},{9,8},{10,11... | collective-permute-start | bytes 18440 | tf_op jit(solution)/shard_map/ppermute | solution.py:532
  307.7 1.2 collective-permute-start.29
  308.2 3.7 collective-permute-start.16
  309.2 5.7 %collective-permute-start.30 = (f32[3,2,256]{2,1,0:T(2,128)S(1)}, f32[3,2,256]{2,1,0:T(2,128)S(1)}, u32[]{:S(2)}, u32[]{:S(2)}) collective-permute-start(f32[3,2,256]{2,1,0:T(2,128)S(1)} %pad_maximum_fusion.19), channel_id=1, source_target_pairs={{0,2},{1,3},{2,0},{3,1},{4,6},{5,7},{6,4},{7,5},{8,10},{9,11},{10,... | collective-permute-start | bytes 18440 | tf_op jit(solution)/shard_map/ppermute | solution.py:532
  314.9 2.0 collective-permute-start.17
  316.3 2.1 collective-permute-start.31
  317.1 14.9 %copy-start.10 = (bf16[256,1024]{1,0:T(8,128)(2,1)}, bf16[256,1024]{1,0:T(8,128)(2,1)S(1)}, u32[]{:S(2)}) copy-start(bf16[256,1024]{1,0:T(8,128)(2,1)S(1)} %fusion.3.sum_ref) | copy-start | bytes 1572868
  317.1 14.9 %collective-permute-start.18 = (bf16[256,1024]{1,0:T(8,128)(2,1)S(1)}, bf16[256,1024]{1,0:T(8,128)(2,1)S(1)}, u32[]{:S(2)}, u32[]{:S(2)}) collective-permute-start(bf16[256,1024]{1,0:T(8,128)(2,1)S(1)} %fusion.3.sum_ref), channel_id=1, source_target_pairs={{0,2},{1,3},{2,0},{3,1},{4,6},{5,7},{6,4},{7,5},{8,10},{9,11},{10,... | collective-permute-start | bytes 1572872 | tf_op jit(solution)/shard_map/ppermute | solution.py:532
  318.6 23.7 %copy-start.8 = (bf16[256,1024]{1,0:T(8,128)(2,1)}, bf16[256,1024]{1,0:T(8,128)(2,1)S(1)}, u32[]{:S(2)}) copy-start(bf16[256,1024]{1,0:T(8,128)(2,1)S(1)} %fusion.1.sum_ref) | copy-start | bytes 1572868
  318.6 23.7 %collective-permute-start.32 = (bf16[256,1024]{1,0:T(8,128)(2,1)S(1)}, bf16[256,1024]{1,0:T(8,128)(2,1)S(1)}, u32[]{:S(2)}, u32[]{:S(2)}) collective-permute-start(bf16[256,1024]{1,0:T(8,128)(2,1)S(1)} %fusion.1.sum_ref), channel_id=1, source_target_pairs={{0,2},{1,3},{2,0},{3,1},{4,6},{5,7},{6,4},{7,5},{8,10},{9,11},{10,... | collective-permute-start | bytes 1572872 | tf_op jit(solution)/shard_map/ppermute | solution.py:532
  336.1 12.8 %collective-permute-start.19 = (bf16[256,1024]{1,0:T(8,128)(2,1)}, bf16[256,1024]{1,0:T(8,128)(2,1)S(1)}, u32[]{:S(2)}, u32[]{:S(2)}) collective-permute-start(bf16[256,1024]{1,0:T(8,128)(2,1)} %get-tuple-element.114.dm_ref), channel_id=1, source_target_pairs={{0,1},{1,0},{2,3},{3,2},{4,5},{5,4},{6,7},{7,6},{8,9},{9,8},{10,11... | collective-permute-start | bytes 1572872 | tf_op jit(solution)/shard_map/ppermute | solution.py:532
  346.5 15.1 %collective-permute-start.33 = (bf16[256,1024]{1,0:T(8,128)(2,1)}, bf16[256,1024]{1,0:T(8,128)(2,1)S(1)}, u32[]{:S(2)}, u32[]{:S(2)}) collective-permute-start(bf16[256,1024]{1,0:T(8,128)(2,1)} %get-tuple-element.137.dm_ref), channel_id=1, source_target_pairs={{0,1},{1,0},{2,3},{3,2},{4,5},{5,4},{6,7},{7,6},{8,9},{9,8},{10,11... | collective-permute-start | bytes 1572872 | tf_op jit(solution)/shard_map/ppermute | solution.py:532
  361.0 12.7 %collective-permute-start.20 = (bf16[256,1024]{1,0:T(8,128)(2,1)}, bf16[256,1024]{1,0:T(8,128)(2,1)S(1)}, u32[]{:S(2)}, u32[]{:S(2)}) collective-permute-start(bf16[256,1024]{1,0:T(8,128)(2,1)} %get-tuple-element.120), channel_id=1, source_target_pairs={{0,1},{1,0},{2,3},{3,2},{4,5},{5,4},{6,7},{7,6},{8,9},{9,8},{10,11... | collective-permute-start | bytes 1572872 | tf_op jit(solution)/shard_map/ppermute | solution.py:532
  373.6 2.2 collective-permute-start.34
  373.8 14.9 %copy-start.7 = (bf16[256,1024]{1,0:T(8,128)(2,1)}, bf16[256,1024]{1,0:T(8,128)(2,1)S(1)}, u32[]{:S(2)}) copy-start(bf16[256,1024]{1,0:T(8,128)(2,1)S(1)} %add_convert_fusion.3.sum_ref) | copy-start | bytes 1572868
  373.9 14.9 %collective-permute-start.21 = (bf16[256,1024]{1,0:T(8,128)(2,1)S(1)}, bf16[256,1024]{1,0:T(8,128)(2,1)S(1)}, u32[]{:S(2)}, u32[]{:S(2)}) collective-permute-start(bf16[256,1024]{1,0:T(8,128)(2,1)S(1)} %add_convert_fusion.3.sum_ref), channel_id=1, source_target_pairs={{0,2},{1,3},{2,0},{3,1},{4,6},{5,7},{6,4},{7,5},{8,10},{9,11},{10,... | collective-permute-start | bytes 1572872 | tf_op jit(solution)/shard_map/ppermute | solution.py:532
  375.9 23.5 %copy-start.6 = (bf16[256,1024]{1,0:T(8,128)(2,1)}, bf16[256,1024]{1,0:T(8,128)(2,1)S(1)}, u32[]{:S(2)}) copy-start(bf16[256,1024]{1,0:T(8,128)(2,1)S(1)} %add_convert_fusion.sum_ref) | copy-start | bytes 1572868
  375.9 23.5 %collective-permute-start.35 = (bf16[256,1024]{1,0:T(8,128)(2,1)S(1)}, bf16[256,1024]{1,0:T(8,128)(2,1)S(1)}, u32[]{:S(2)}, u32[]{:S(2)}) collective-permute-start(bf16[256,1024]{1,0:T(8,128)(2,1)S(1)} %add_convert_fusion.sum_ref), channel_id=1, source_target_pairs={{0,2},{1,3},{2,0},{3,1},{4,6},{5,7},{6,4},{7,5},{8,10},{9,11},{10,... | collective-permute-start | bytes 1572872 | tf_op jit(solution)/shard_map/ppermute | solution.py:532
  393.4 13.8 %copy-start.41 = (f32[16,1024]{1,0:T(8,128)S(1)}, f32[16,1024]{1,0:T(8,128)}, u32[]{:S(2)}) copy-start(f32[16,1024]{1,0:T(8,128)} %get-tuple-element.161) | copy-start | bytes 196612
  393.4 13.8 %collective-permute-start.22 = (bf16[256,1024]{1,0:T(8,128)(2,1)}, bf16[256,1024]{1,0:T(8,128)(2,1)S(1)}, u32[]{:S(2)}, u32[]{:S(2)}) collective-permute-start(bf16[256,1024]{1,0:T(8,128)(2,1)} %get-tuple-element.122.dm_ref), channel_id=1, source_target_pairs={{0,1},{1,0},{2,3},{3,2},{4,5},{5,4},{6,7},{7,6},{8,9},{9,8},{10,11... | collective-permute-start | bytes 1572872 | tf_op jit(solution)/shard_map/ppermute | solution.py:532
  404.1 8.1 %collective-permute-start.36 = (bf16[256,1024]{1,0:T(8,128)(2,1)}, bf16[256,1024]{1,0:T(8,128)(2,1)S(1)}, u32[]{:S(2)}, u32[]{:S(2)}) collective-permute-start(bf16[256,1024]{1,0:T(8,128)(2,1)} %get-tuple-element.145.dm_ref), channel_id=1, source_target_pairs={{0,1},{1,0},{2,3},{3,2},{4,5},{5,4},{6,7},{7,6},{8,9},{9,8},{10,11... | collective-permute-start | bytes 1572872 | tf_op jit(solution)/shard_map/ppermute | solution.py:532
  417.1 16.1 %copy-start.43 = (f32[16,1024]{1,0:T(8,128)S(1)}, f32[16,1024]{1,0:T(8,128)}, u32[]{:S(2)}) copy-start(f32[16,1024]{1,0:T(8,128)} %get-tuple-element.158) | copy-start | bytes 196612
  417.2 16.1 %copy-start.44 = (f32[16,1024]{1,0:T(8,128)S(1)}, f32[16,1024]{1,0:T(8,128)}, u32[]{:S(2)}) copy-start(f32[16,1024]{1,0:T(8,128)} %get-tuple-element.159) | copy-start | bytes 196612
  417.2 18.1 %copy-start.36 = (f32[16,1024]{1,0:T(8,128)S(1)}, f32[16,1024]{1,0:T(8,128)}, u32[]{:S(2)}) copy-start(f32[16,1024]{1,0:T(8,128)} %get-tuple-element.165) | copy-start | bytes 196612
  417.2 18.1 %copy-start.38 = (f32[16,1024]{1,0:T(8,128)S(1)}, f32[16,1024]{1,0:T(8,128)}, u32[]{:S(2)}) copy-start(f32[16,1024]{1,0:T(8,128)} %get-tuple-element.166) | copy-start | bytes 196612
  417.2 18.1 %copy-start.35 = (f32[16,1024]{1,0:T(8,128)S(1)}, f32[16,1024]{1,0:T(8,128)}, u32[]{:S(2)}) copy-start(f32[16,1024]{1,0:T(8,128)} %get-tuple-element.167) | copy-start | bytes 196612
  417.2 18.1 %copy-start.37 = (f32[16,1024]{1,0:T(8,128)S(1)}, f32[16,1024]{1,0:T(8,128)}, u32[]{:S(2)}) copy-start(f32[16,1024]{1,0:T(8,128)} %get-tuple-element.168) | copy-start | bytes 196612
  417.2 19.7 %copy-start.45 = (f32[16,256]{1,0:T(8,128)S(1)}, f32[16,256]{1,0:T(8,128)}, u32[]{:S(2)}) copy-start(f32[16,256]{1,0:T(8,128)} %get-tuple-element.163) | copy-start | bytes 49156
  417.2 19.7 %copy-start.46 = (f32[16,256]{1,0:T(8,128)S(1)}, f32[16,256]{1,0:T(8,128)}, u32[]{:S(2)}) copy-start(f32[16,256]{1,0:T(8,128)} %get-tuple-element.164) | copy-start | bytes 49156
  433.3 2.0 collective-permute-start.37
  435.4 3.9 collective-permute-start.38
  439.4 4.4 collective-permute-start.39
  443.8 4.4 collective-permute-start.40
  448.3 6.6 %collective-permute-start.41 = (f32[4,4736]{1,0:T(4,128)S(1)}, f32[4,4736]{1,0:T(4,128)S(1)}, u32[]{:S(2)}, u32[]{:S(2)}) collective-permute-start(f32[4,4736]{1,0:T(4,128)S(1)} %add.371), channel_id=1, source_target_pairs={{0,16},{4,20},{8,24},{12,28},{16,0},{20,4},{24,8},{28,12},{1,17},{... | collective-permute-start | bytes 227336 | tf_op jit(solution)/shard_map/ppermute | solution.py:532
  455.0 4.4 collective-permute-start.42
  459.4 1.4 collective-permute-start.43
  (32 other events, 114.7 us)
